TPU v7x, 32 devices: a whole 2x2x4 slice. The times are simulated.
32 devices in a mesh: stream: 8 (over z, y), span: 4 (over x, core).
Axes of the slice: x: 2, y: 2, z: 4, core: 2. Of those that a mesh axis runs over, the one named last changes fastest.
Arguments:
- right_sides: bfloat16 [8, 4, 4, 512, 128], P('stream', 'span'), may hold values from -2.5 to 2.5
- inverse: bfloat16 [8, 4, 4, 512, 512], P('stream', 'span'), as said below
- coupling: bfloat16 [8, 4, 4, 3, 64, 512], P('stream', 'span')
- sweep_order: int32 [8, 4, 4], P('stream', 'span'), may hold values from 0 to 3, each once within a row
Outputs:
- solution: bfloat16 [8, 4, 4, 512, 128], P('stream', 'span')
Inputs may be any that keep to these rules, and one draw needn't show every extreme that they name: `sweep_order`: each group's 4 slots appear once each. Every diagonal block's inverse is well conditioned and of order one.
All inputs are finite; a program needn't handle non-finite values.
Results may differ from a plain program's by a relative error of at most 0.024.
Values may be sent and summed in bfloat16 or wider, within the bound.
No kernel may reach another device: no remote copies, remote signals or barrier semaphores. Data moves between devices by JAX's collectives and lax.ppermute only.
A program may use at most 64 MiB of HBM per device.

v0:
```python
import jax
import jax.numpy as jnp
from jax import lax
from jax.sharding import PartitionSpec as P

NP = 8
SWEEPS = 6


def prefix_2(value, axis, join, neutral):
    place = lax.axis_index(axis)
    gathered = jax.tree.map(
        lambda a, kind: lax.all_gather(a.astype(kind), axis), value, (jnp.bfloat16, jnp.bfloat16)
    )
    state = jax.tree.map(lambda a, e: jnp.zeros_like(a) + jnp.asarray(e, a.dtype), value, neutral)

    def one(step, state):
        return join(
            state,
            jax.tree.map(
                lambda a, own: lax.dynamic_index_in_dim(a, step, 0, False).astype(own.dtype),
                gathered,
                value,
            ),
        )

    return lax.fori_loop(0, place, one, state)


def padded(block, sides, width):
    for axis, dim in sides:
        count = lax.axis_size(axis)
        forward = [(i, i + 1) for i in range(count - 1)]
        backward = [(target, source) for source, target in forward]
        low = lax.ppermute(
            lax.slice_in_dim(block, block.shape[dim] - width, None, axis=dim), axis, forward
        )
        high = lax.ppermute(lax.slice_in_dim(block, 0, width, axis=dim), axis, backward)
        block = jnp.concatenate([low, block, high], axis=dim)
    return block


def exact_dot(left, right):
    return jnp.dot(left, right, precision=lax.Precision.HIGHEST, preferred_element_type=jnp.float32)


def transposed_dot(coupling_rows, values):
    return lax.dot_general(
        coupling_rows, values, (((0,), (0,)), ((), ())), preferred_element_type=jnp.float32
    )


def face_rows(values, layer):
    columns = values.shape[-1]
    return values.reshape(NP, NP, NP, columns)[:, layer].reshape(NP * NP, columns)


def chain_combine(earlier, later_part):
    return (
        exact_dot(later_part[0], earlier[0]),
        exact_dot(later_part[0], earlier[1]) + later_part[1],
    )


def advance(entry, gained, liftings, transfers, nodes, face):
    trace_now = entry
    pieces = []
    for position in range(len(gained)):
        pieces.append(
            (gained[position] + exact_dot(liftings[position], trace_now)).astype(jnp.bfloat16)
        )
        trace_now = exact_dot(transfers[position], trace_now) + gained[position][nodes - face :]
    return pieces


def shards(right_sides, inverse, coupling, sweep_order):
    right_sides = right_sides[0, 0]
    inverse = inverse[0, 0]
    coupling = coupling[0, 0]
    sweep_order = sweep_order[0, 0]
    count = inverse.shape[0]
    nodes = inverse.shape[1]
    face = coupling.shape[2]
    width = right_sides.shape[2]

    def picked(values, position):
        return lax.dynamic_index_in_dim(values, sweep_order[position], 0, keepdims=False)

    inverses = [picked(inverse, position) for position in range(count)]
    couplings = [picked(coupling, position) for position in range(count)]
    givens = [picked(right_sides, position) for position in range(count)]
    liftings = [
        lax.dot_general(
            inverses[position],
            couplings[position][0],
            (((1,), (1,)), ((), ())),
            preferred_element_type=jnp.float32,
        )
        for position in range(count)
    ]
    transfers = [lifting[nodes - face :] for lifting in liftings]
    identity_map = jnp.eye(face, dtype=jnp.float32)
    composite = identity_map
    entry_maps = []
    for position in range(count):
        entry_maps.append(composite)
        composite = exact_dot(transfers[position], composite)
    lower_faces = None
    upper_faces = None
    solution = None
    for sweep_index in range(SWEEPS):
        last_sweep = sweep_index == SWEEPS - 1
        gained = []
        for position in range(count):
            source = givens[position].astype(jnp.float32)
            if lower_faces is not None:
                source = source + transposed_dot(couplings[position][1], lower_faces[position])
                source = source + transposed_dot(couplings[position][2], upper_faces[position])
            gained.append(
                jnp.dot(
                    inverses[position],
                    source.astype(jnp.bfloat16),
                    preferred_element_type=jnp.float32,
                )
            )
        offset = jnp.zeros((face, width), jnp.float32)
        offsets = []
        for position in range(count):
            offsets.append(offset)
            offset = exact_dot(transfers[position], offset) + gained[position][nodes - face :]
        prefix = prefix_2(
            (composite, offset), "stream", chain_combine, (identity_map, jnp.zeros_like(offset))
        )
        entry = prefix[1]
        solution = advance(entry, gained, liftings, transfers, nodes, face)
        if not last_sweep:
            stacked = jnp.stack(
                [
                    jnp.stack([face_rows(piece, layer) for piece in solution])
                    for layer in (0, NP - 1)
                ]
            )
            neighbours = padded(stacked, (("span", 0),), 1)
            lower_faces = [neighbours[0, position] for position in range(count)]
            upper_faces = [neighbours[3, position] for position in range(count)]
    placed = jnp.zeros((count, nodes, width), jnp.bfloat16)
    for position in range(count):
        placed = lax.dynamic_update_index_in_dim(
            placed, solution[position], sweep_order[position], 0
        )
    return placed[None, None]


def solution(mesh):
    in_specs = (
        P("stream", "span", None, None, None),
        P("stream", "span", None, None, None),
        P("stream", "span", None, None, None, None),
        P("stream", "span", None),
    )
    out_specs = P("stream", "span", None, None, None)
    return jax.shard_map(shards, mesh=mesh, in_specs=in_specs, out_specs=out_specs, check_vma=False)
```

profile of v0, /device:TPU:0, one launch (start us, length us, event | category | flops | bytes accessed | tf_op | source)
XLA Modules:
  0.0 413.7 jit_solution(16662047948575342929)
XLA Ops:
  19.9 32.3 %all-gather = bf16[512,64]{1,0:T(8,128)(2,1)S(1)} all-gather(bf16[64,64]{1,0:T(8,128)(2,1)S(1)} %convolution_convert_fusion), channel_id=2, replica_groups=mesh['stream'=8,'span'=4] {'stream'}, dimensions={0}, use_global_device_ids=true | all-gather | bytes 73728 | tf_op jit(solution)/shard_map/all_gather | solution.py:13
  55.5 30.5 %all-gather.1 = bf16[512,128]{1,0:T(8,128)(2,1)S(1)} all-gather(bf16[64,128]{1,0:T(8,128)(2,1)S(1)} %fusion.110), channel_id=3, replica_groups=mesh['stream'=8,'span'=4] {'stream'}, dimensions={0}, use_global_device_ids=true | all-gather | bytes 147456 | tf_op jit(solution)/shard_map/all_gather | solution.py:13
  95.9 3.0 collective-permute-start
  114.7 2.2 fusion.106
  117.9 31.3 %all-gather.2 = bf16[512,128]{1,0:T(8,128)(2,1)S(1)} all-gather(bf16[64,128]{1,0:T(8,128)(2,1)S(1)} %fusion.247), channel_id=4, replica_groups=mesh['stream'=8,'span'=4] {'stream'}, dimensions={0}, use_global_device_ids=true | all-gather | bytes 147456 | tf_op jit(solution)/shard_map/all_gather | solution.py:13
  159.2 3.0 collective-permute-start.2
  168.0 2.2 fusion.105
  178.0 2.2 fusion.102
  181.3 31.9 %all-gather.3 = bf16[512,128]{1,0:T(8,128)(2,1)S(1)} all-gather(bf16[64,128]{1,0:T(8,128)(2,1)S(1)} %fusion.246), channel_id=5, replica_groups=mesh['stream'=8,'span'=4] {'stream'}, dimensions={0}, use_global_device_ids=true | all-gather | bytes 147456 | tf_op jit(solution)/shard_map/all_gather | solution.py:13
  223.3 3.0 collective-permute-start.4
  229.9 2.2 fusion.100
  242.1 2.2 fusion.98
  245.4 31.8 %all-gather.4 = bf16[512,128]{1,0:T(8,128)(2,1)S(1)} all-gather(bf16[64,128]{1,0:T(8,128)(2,1)S(1)} %fusion.245), channel_id=6, replica_groups=mesh['stream'=8,'span'=4] {'stream'}, dimensions={0}, use_global_device_ids=true | all-gather | bytes 147456 | tf_op jit(solution)/shard_map/all_gather | solution.py:13
  287.2 3.0 collective-permute-start.6
  293.7 2.2 fusion.96
  295.9 2.2 fusion.97
  306.0 2.2 fusion.94
  309.2 31.8 %all-gather.5 = bf16[512,128]{1,0:T(8,128)(2,1)S(1)} all-gather(bf16[64,128]{1,0:T(8,128)(2,1)S(1)} %fusion.244), channel_id=7, replica_groups=mesh['stream'=8,'span'=4] {'stream'}, dimensions={0}, use_global_device_ids=true | all-gather | bytes 147456 | tf_op jit(solution)/shard_map/all_gather | solution.py:13
  351.0 3.3 collective-permute-start.8
  357.8 2.2 fusion.93
  360.0 2.2 fusion.92
  365.0 2.2 fusion.91
  370.1 2.2 fusion.90
  373.4 31.8 %all-gather.6 = bf16[512,128]{1,0:T(8,128)(2,1)S(1)} all-gather(bf16[64,128]{1,0:T(8,128)(2,1)S(1)} %fusion.243), channel_id=8, replica_groups=mesh['stream'=8,'span'=4] {'stream'}, dimensions={0}, use_global_device_ids=true | all-gather | bytes 147456 | tf_op jit(solution)/shard_map/all_gather | solution.py:13
  (178 shorter events, 142.2 us)
Async XLA Ops:
  0.0 7.0 %copy-start = (bf16[1,1,4,512,512]{4,3,2,1,0:T(8,128)(2,1)S(1)}, bf16[1,1,4,512,512]{4,3,2,1,0:T(8,128)(2,1)}, u32[]{:S(2)}) copy-start(bf16[1,1,4,512,512]{4,3,2,1,0:T(8,128)(2,1)} %param.17) | copy-start | bytes 6291460
  0.0 14.1 %copy-start.1 = (bf16[1,1,4,512,128]{4,3,2,1,0:T(8,128)(2,1)S(1)}, bf16[1,1,4,512,128]{4,3,2,1,0:T(8,128)(2,1)}, u32[]{:S(2)}) copy-start(bf16[1,1,4,512,128]{4,3,2,1,0:T(8,128)(2,1)} %param.16) | copy-start | bytes 1572868
  86.0 7.9 %copy-start.8 = (f32[512,128]{1,0:T(8,128)S(1)}, f32[512,128]{1,0:T(8,128)}, u32[]{:S(2)}) copy-start(f32[512,128]{1,0:T(8,128)} %fusion.134) | copy-start | bytes 786436
  94.6 4.4 %collective-permute-start.1 = (bf16[1,4,64,128]{3,2,1,0:T(8,128)(2,1)S(1)}, bf16[1,4,64,128]{3,2,1,0:T(8,128)(2,1)}, u32[]{:S(2)}, u32[]{:S(2)}) collective-permute-start(bf16[1,4,64,128]{3,2,1,0:T(8,128)(2,1)S(1)} %maximum_bitcast_fusion.1), channel_id=1, source_target_pairs={{1,0},{2,1},{3,2},{5,4},{6,5},{7,6},{9,8},{10,9},{11,10},{13,12},{... | collective-permute-start | bytes 196616 | tf_op jit(solution)/shard_map/ppermute | solution.py:38
  95.9 6.6 %collective-permute-start = (bf16[1,4,64,128]{3,2,1,0:T(8,128)(2,1)S(1)}, bf16[1,4,64,128]{3,2,1,0:T(8,128)(2,1)S(1)}, u32[]{:S(2)}, u32[]{:S(2)}) collective-permute-start(bf16[1,4,64,128]{3,2,1,0:T(8,128)(2,1)S(1)} %maximum_bitcast_fusion), channel_id=1, source_target_pairs={{0,1},{1,2},{2,3},{4,5},{5,6},{6,7},{8,9},{9,10},{10,11},{12,13},{... | collective-permute-start | bytes 196616 | tf_op jit(solution)/shard_map/ppermute | solution.py:35
  149.3 7.9 %copy-start.4 = (f32[512,128]{1,0:T(8,128)S(1)}, f32[512,128]{1,0:T(8,128)}, u32[]{:S(2)}) copy-start(f32[512,128]{1,0:T(8,128)} %fusion.106) | copy-start | bytes 786436
  157.9 4.4 %collective-permute-start.3 = (bf16[1,4,64,128]{3,2,1,0:T(8,128)(2,1)S(1)}, bf16[1,4,64,128]{3,2,1,0:T(8,128)(2,1)S(1)}, u32[]{:S(2)}, u32[]{:S(2)}) collective-permute-start(bf16[1,4,64,128]{3,2,1,0:T(8,128)(2,1)S(1)} %maximum_bitcast_fusion.3), channel_id=1, source_target_pairs={{1,0},{2,1},{3,2},{5,4},{6,5},{7,6},{9,8},{10,9},{11,10},{13,12},{... | collective-permute-start | bytes 196616 | tf_op jit(solution)/shard_map/ppermute | solution.py:38
  159.2 6.6 %collective-permute-start.2 = (bf16[1,4,64,128]{3,2,1,0:T(8,128)(2,1)S(1)}, bf16[1,4,64,128]{3,2,1,0:T(8,128)(2,1)S(1)}, u32[]{:S(2)}, u32[]{:S(2)}) collective-permute-start(bf16[1,4,64,128]{3,2,1,0:T(8,128)(2,1)S(1)} %maximum_bitcast_fusion.2), channel_id=1, source_target_pairs={{0,1},{1,2},{2,3},{4,5},{5,6},{6,7},{8,9},{9,10},{10,11},{12,13},{... | collective-permute-start | bytes 196616 | tf_op jit(solution)/shard_map/ppermute | solution.py:35
  213.4 7.9 %copy-start.5 = (f32[512,128]{1,0:T(8,128)S(1)}, f32[512,128]{1,0:T(8,128)}, u32[]{:S(2)}) copy-start(f32[512,128]{1,0:T(8,128)} %fusion.102) | copy-start | bytes 786436
  222.0 4.4 %collective-permute-start.5 = (bf16[1,4,64,128]{3,2,1,0:T(8,128)(2,1)S(1)}, bf16[1,4,64,128]{3,2,1,0:T(8,128)(2,1)S(1)}, u32[]{:S(2)}, u32[]{:S(2)}) collective-permute-start(bf16[1,4,64,128]{3,2,1,0:T(8,128)(2,1)S(1)} %maximum_bitcast_fusion.5), channel_id=1, source_target_pairs={{1,0},{2,1},{3,2},{5,4},{6,5},{7,6},{9,8},{10,9},{11,10},{13,12},{... | collective-permute-start | bytes 196616 | tf_op jit(solution)/shard_map/ppermute | solution.py:38
  223.3 6.6 %collective-permute-start.4 = (bf16[1,4,64,128]{3,2,1,0:T(8,128)(2,1)S(1)}, bf16[1,4,64,128]{3,2,1,0:T(8,128)(2,1)S(1)}, u32[]{:S(2)}, u32[]{:S(2)}) collective-permute-start(bf16[1,4,64,128]{3,2,1,0:T(8,128)(2,1)S(1)} %maximum_bitcast_fusion.4), channel_id=1, source_target_pairs={{0,1},{1,2},{2,3},{4,5},{5,6},{6,7},{8,9},{9,10},{10,11},{12,13},{... | collective-permute-start | bytes 196616 | tf_op jit(solution)/shard_map/ppermute | solution.py:35
  277.2 7.9 %copy-start.6 = (f32[512,128]{1,0:T(8,128)S(1)}, f32[512,128]{1,0:T(8,128)}, u32[]{:S(2)}) copy-start(f32[512,128]{1,0:T(8,128)} %fusion.98) | copy-start | bytes 786436
  285.8 4.4 %collective-permute-start.7 = (bf16[1,4,64,128]{3,2,1,0:T(8,128)(2,1)S(1)}, bf16[1,4,64,128]{3,2,1,0:T(8,128)(2,1)S(1)}, u32[]{:S(2)}, u32[]{:S(2)}) collective-permute-start(bf16[1,4,64,128]{3,2,1,0:T(8,128)(2,1)S(1)} %maximum_bitcast_fusion.7), channel_id=1, source_target_pairs={{1,0},{2,1},{3,2},{5,4},{6,5},{7,6},{9,8},{10,9},{11,10},{13,12},{... | collective-permute-start | bytes 196616 | tf_op jit(solution)/shard_map/ppermute | solution.py:38
  287.2 6.6 %collective-permute-start.6 = (bf16[1,4,64,128]{3,2,1,0:T(8,128)(2,1)S(1)}, bf16[1,4,64,128]{3,2,1,0:T(8,128)(2,1)S(1)}, u32[]{:S(2)}, u32[]{:S(2)}) collective-permute-start(bf16[1,4,64,128]{3,2,1,0:T(8,128)(2,1)S(1)} %maximum_bitcast_fusion.6), channel_id=1, source_target_pairs={{0,1},{1,2},{2,3},{4,5},{5,6},{6,7},{8,9},{9,10},{10,11},{12,13},{... | collective-permute-start | bytes 196616 | tf_op jit(solution)/shard_map/ppermute | solution.py:35
  341.1 7.9 %copy-start.7 = (f32[512,128]{1,0:T(8,128)S(1)}, f32[512,128]{1,0:T(8,128)}, u32[]{:S(2)}) copy-start(f32[512,128]{1,0:T(8,128)} %fusion.94) | copy-start | bytes 786436
  349.7 4.6 %collective-permute-start.9 = (bf16[1,4,64,128]{3,2,1,0:T(8,128)(2,1)S(1)}, bf16[1,4,64,128]{3,2,1,0:T(8,128)(2,1)S(1)}, u32[]{:S(2)}, u32[]{:S(2)}) collective-permute-start(bf16[1,4,64,128]{3,2,1,0:T(8,128)(2,1)S(1)} %maximum_bitcast_fusion.9), channel_id=1, source_target_pairs={{1,0},{2,1},{3,2},{5,4},{6,5},{7,6},{9,8},{10,9},{11,10},{13,12},{... | collective-permute-start | bytes 196616 | tf_op jit(solution)/shard_map/ppermute | solution.py:38
  351.0 6.8 %collective-permute-start.8 = (bf16[1,4,64,128]{3,2,1,0:T(8,128)(2,1)S(1)}, bf16[1,4,64,128]{3,2,1,0:T(8,128)(2,1)S(1)}, u32[]{:S(2)}, u32[]{:S(2)}) collective-permute-start(bf16[1,4,64,128]{3,2,1,0:T(8,128)(2,1)S(1)} %maximum_bitcast_fusion.8), channel_id=1, source_target_pairs={{0,1},{1,2},{2,3},{4,5},{5,6},{6,7},{8,9},{9,10},{10,11},{12,13},{... | collective-permute-start | bytes 196616 | tf_op jit(solution)/shard_map/ppermute | solution.py:35
  372.3 38.4 %copy-start.2 = (f32[512,128]{1,0:T(8,128)S(1)}, f32[512,128]{1,0:T(8,128)}, u32[]{:S(2)}) copy-start(f32[512,128]{1,0:T(8,128)} %fusion.91) | copy-start | bytes 786436
  405.2 7.3 %copy-start.3 = (f32[512,128]{1,0:T(8,128)S(1)}, f32[512,128]{1,0:T(8,128)}, u32[]{:S(2)}) copy-start(f32[512,128]{1,0:T(8,128)} %fusion.90) | copy-start | bytes 786436
  411.7 0.8 copy-start.9
where the time goes:
time: 419 us; the launch traced here: 414 us
  blocking collectives  222 us (53%)
  matrix products  159 us (38%)
  starting transfers between devices  21.9 us (5%)
  between operations  8.32 us (2%)
    all_gather x7, blocking collectives, prefix_2(): lax.all_gather(a.astype(kind), axis)  222 us
    dot_general x65, matrix products, exact_dot(): jnp.dot(left, right, precision=lax.Precision.HIGHEST, preferred_element_t...  70.7 us
    dot_general x24, matrix products, shards(): jnp.dot(inverses[position], source.astype(jnp.bfloat16), preferred_elemen...  48.6 us
    dot_general x20, matrix products, transposed_dot(): lax.dot_general(coupling_rows, values, (((0,), (0,)), ((), ())), preferre...  35.3 us
    ppermute x5, starting transfers between devices, padded(): lax.ppermute(lax.slice_in_dim(block, block.shape[dim] - width, None, axis...  15.4 us
  transfers between devices with their start and end apart: 10, of which 0 were waited for; matrix products, arithmetic and copies ran while one was open for 4% of the time, Pallas kernels for 0%

commit v1 on v0

v1 whole, which is shorter than its diff:
```python
import functools

import jax
import jax.numpy as jnp
from jax import lax
from jax.experimental import pallas as pl
from jax.experimental.pallas import tpu as pltpu
from jax.sharding import PartitionSpec as P

NP = 8
SWEEPS = 6
VMEM = pl.BlockSpec(memory_space=pltpu.VMEM)
SMEM = pl.BlockSpec(memory_space=pltpu.SMEM)
F32 = jnp.float32
BF16 = jnp.bfloat16


def bits_of(count):
    return [1 << i for i in range(count.bit_length() - 1)]


def reversed_bits(value, count):
    bits = bits_of(count)
    total = 0
    for low, high in zip(bits, bits[::-1]):
        total = total + jnp.where((value & low) != 0, high, 0)
    return total


def reversed_static(value, count):
    bits = bits_of(count)
    return sum(high for low, high in zip(bits, bits[::-1]) if value & low)


def swap(value, axis, mask):
    count = lax.axis_size(axis)
    return lax.ppermute(value, axis, [(i, i ^ mask) for i in range(count)])


def dot(left, right):
    return jnp.dot(left, right, preferred_element_type=F32)


def dot_nt(left, right):
    return lax.dot_general(left, right, (((1,), (1,)), ((), ())), preferred_element_type=F32)


def lane_is_low(shape, face):
    return lax.broadcasted_iota(jnp.int32, shape, len(shape) - 1) < face


def facemap_kernel(place, order, inverse, coupling, given, maps, gains, *, groups):
    count, nodes, width = given.shape
    face = coupling.shape[1] // 3
    part = nodes // NP
    layer = part // NP
    share = width // groups
    outs = []
    for p in range(count):
        slot = order[p]
        lower = []
        upper = []
        for a in range(NP):
            head = inverse[slot, a * part : a * part + 2 * layer, :].astype(F32)
            tail = inverse[slot, (a + 1) * part - 2 * layer : (a + 1) * part, :].astype(F32)
            lower.append(head[:layer])
            upper.append(tail[layer:])
        faces = jnp.concatenate(lower + upper, axis=0).astype(BF16)
        outflow = inverse[slot, nodes - face :, :]
        blank = jnp.zeros_like(outflow)
        pair = [outflow, blank] if p % 2 == 0 else [blank, outflow]
        rows = jnp.concatenate([faces] + pair, axis=0)
        full = dot_nt(coupling[slot], rows)
        full = jnp.concatenate([full[2 * face :], full[face : 2 * face], full[:face]], axis=0)
        maps[p * 3 * face : (p + 1) * 3 * face, :] = full[:, : 2 * face].astype(BF16)
        outs.append(full[:, 2 * face :])
        if p % 2 == 1:
            at = (count + p // 2) * 3 * face
            maps[at : at + 3 * face, :] = (outs[p - 1] + outs[p]).astype(BF16)
        gain = dot(rows, given[slot]).T.astype(BF16)
        for j in range(groups):
            gains[place[0] ^ j, p] = gain[j * share : (j + 1) * share]


def unpack_maps(map_refs, weights, count, face):
    shape = (3 * face, 2 * face)
    low = lane_is_low(shape, face)
    blank = jnp.zeros((face, 4 * face), BF16)
    for pos, ref in enumerate(map_refs):
        for p in range(count):
            sides = ref[p * 3 * face : (p + 1) * 3 * face, :]
            at = (count + p // 2) * 3 * face
            outs = ref[at : at + 3 * face, :]
            outs = jnp.where(low if p % 2 == 0 else jnp.logical_not(low), outs, jnp.zeros_like(outs))
            full = jnp.concatenate([sides, outs], axis=1)
            weights[pos, p, : 2 * face, :] = full[: 2 * face]
            inflow_at = (2 + (p + 1) % 2) * face
            other_at = (2 + p % 2) * face
            weights[pos, p, inflow_at : inflow_at + face, :] = full[2 * face :]
            weights[pos, p, other_at : other_at + face, :] = blank


def sweep_step(me, pos, now, before, groups, count, face, share, weights, gains, states, inflow, keep=None):
    own = me ^ reversed_bits(pos, groups)
    below = jnp.where(own > 0, reversed_bits((own - 1) & (groups - 1) ^ me, groups), groups)
    above = jnp.where(own < groups - 1, reversed_bits((own + 1) & (groups - 1) ^ me, groups), groups)
    rel = reversed_bits(pos, groups)
    entry = inflow
    out = None
    for p in range(count):
        upper = states[before, above, p]
        lower = states[before, below, p]
        lag = jnp.where(lane_is_low(upper.shape, face), upper, lower)
        if keep is not None:
            keep(p, lag, entry)
        result = dot(jnp.concatenate([lag, entry], axis=1), weights[pos, p])
        head = result[:share] + gains[rel, p].astype(F32)
        result = head if result.shape[0] == share else jnp.concatenate([head, result[share:]], axis=0)
        states[now, pos, p] = result[:, : 2 * face].astype(BF16)
        out = result[:, 2 * face :]
        entry = out.astype(BF16)
    return out


def respond_kernel(place, *refs, groups, count, face):
    map_refs = refs[:groups]
    gains, response, offset, weights, states, unit = refs[groups:]
    me = place[0]
    share = gains.shape[2]
    rows = states.shape[3]
    half = groups // 2
    unpack_maps(map_refs, weights, count, face)
    states[...] = jnp.zeros_like(states)
    unit[...] = jnp.zeros_like(unit)
    row = lax.broadcasted_iota(jnp.int32, (rows, 2 * face), 0) - share
    lane = lax.broadcasted_iota(jnp.int32, (rows, 2 * face), 1) - face
    for pos in range(half):
        hit = jnp.logical_and(lane >= 0, row == lane + pos * face)
        unit[0, pos] = jnp.where(hit, 1.0, 0.0).astype(BF16)

    def sweep(k, carry):
        now = k % 2
        before = 1 - now

        def tiles(t):
            ends = []
            for pos in (2 * t, 2 * t + 1, 2 * t + half, 2 * t + half + 1):
                inflow = unit[jnp.minimum(k, 1), pos]
                ends.append(
                    sweep_step(me, pos, now, before, groups, count, face, share, weights, gains, states, inflow)
                )
            even = pltpu.roll(ends[0], face, 1) + ends[1]
            odd = pltpu.roll(ends[2], face, 1) + ends[3]
            return even, odd

        def put(t, even, odd):
            at = t * 2 * face
            offset[k, :, pl.ds(at, 2 * face)] = even[:share].astype(BF16)
            offset[k, :, pl.ds(half * face + at, 2 * face)] = odd[:share].astype(BF16)
            response[k, :, pl.ds(at, 2 * face)] = (even[share:] + odd[share:]).astype(BF16)

        if groups == 4:
            put(0, *tiles(0))
        else:

            def block(t, inner):
                even, odd = tiles(t)
                put(pl.multiple_of(t, 1), even, odd)
                return inner

            lax.fori_loop(0, groups // 4, block, 0)
        return carry

    lax.fori_loop(0, SWEEPS, sweep, 0)


def pick(flag, first, second):
    return jnp.where(flag != 0, first, second)


def compose_kernel(flag, own_even, own_odd, got_even, got_odd, own_offset, got_offset, response, offset):
    down = flag[0]
    width = own_even.shape[1]
    upper = []
    for k in range(SWEEPS):
        upper.append(
            (pick(down, own_even[k], got_even[k]), pick(down, own_odd[k], got_odd[k]))
        )
    first = [pick(down, got_even[k], own_even[k]) for k in range(SWEEPS)]
    for m in range(SWEEPS):
        total = None
        for j in range(m + 1):
            term = dot(first[j], upper[m - j][j % 2])
            total = term if total is None else total + term
        response[m] = total.astype(BF16)
    inner = [pick(down, got_offset[k], own_offset[k]) for k in range(SWEEPS)]
    for k in range(SWEEPS):
        total = pick(down, own_offset[k], got_offset[k]).astype(F32)
        total = total + through(inner, upper, k, width)
        offset[k] = total.astype(BF16)


def through(inner, maps, k, width):
    parts = [None, None]
    for m in range(k + 1):
        value = inner[k - m]
        for group in (0, 1):
            term = dot(value[:, group * width : (group + 1) * width], maps[m][group])
            target = (group + m) % 2
            parts[target] = term if parts[target] is None else parts[target] + term
    return jnp.concatenate(parts, axis=1)


def resolve_kernel(place, flags, *refs, groups, count, face, levels):
    map_refs = refs[:groups]
    gains = refs[groups]
    top = refs[groups + 1]
    lower = refs[groups + 2 : groups + 2 + 3 * levels]
    wanted, weights, states, inflows = refs[groups + 2 + 3 * levels :]
    me = place[0]
    share = gains.shape[2]
    half = groups // 2
    width = half * face
    unpack_maps(map_refs, weights, count, face)
    states[...] = jnp.zeros_like(states)
    values = [pick(flags[levels], top[k], jnp.zeros_like(top[k])) for k in range(SWEEPS)]
    for level in range(levels - 1, -1, -1):
        even, odd, offset = lower[3 * level : 3 * level + 3]
        maps = [(even[k], odd[k]) for k in range(SWEEPS)]
        moved = [
            (offset[k].astype(F32) + through(values, maps, k, width)).astype(BF16) for k in range(SWEEPS)
        ]
        values = [pick(flags[level], moved[k], values[k]) for k in range(SWEEPS)]
    for k in range(SWEEPS):
        for tile in range(half):
            both = values[k][:, tile * 2 * face : (tile + 1) * 2 * face]
            inflows[k, 2 * tile] = pltpu.roll(both.astype(F32), face, 1).astype(BF16)
            inflows[k, 2 * tile + 1] = both

    def sweep(k, carry):
        now = k % 2
        before = 1 - now

        def group(pos):
            rel = reversed_bits(pos, groups)
            kept = []

            def keep(p, lag, entry):
                wanted[rel, p] = lag
                kept.append(entry)
                if p % 2 == 1:
                    low = lane_is_low(entry.shape, face)
                    wanted[rel, count + p // 2] = jnp.where(low, kept[p], kept[p - 1])

            sweep_step(
                me, pos, now, before, groups, count, face, share, weights, gains, states, inflows[k, pos], keep
            )

        if groups == 4:
            for pos in range(groups):
                group(pos)
        else:

            def block(pos, inner):
                group(pos)
                return inner

            lax.fori_loop(0, groups, block, 0)
        return carry

    lax.fori_loop(0, SWEEPS, sweep, 0)


def final_kernel(place, order, inverse, coupling, given, wanted, placed, gathered, *, groups):
    count, nodes, width = given.shape
    face = coupling.shape[1] // 3
    share = width // groups
    for rel in range(groups):
        at = pl.multiple_of((place[0] ^ rel) * share, share)
        for m in range(wanted.shape[1]):
            gathered[m, pl.ds(at, share), :] = wanted[rel, m].astype(F32)
    for p in range(count):
        slot = order[p]
        rows = coupling[slot]
        blank = jnp.zeros((face, nodes), BF16)
        inflow_rows = rows[:face]
        pair = [blank, inflow_rows] if p % 2 == 0 else [inflow_rows, blank]
        sides = jnp.concatenate([rows[2 * face :], rows[face : 2 * face]] + pair, axis=0)
        traces = jnp.concatenate([gathered[p], gathered[count + p // 2]], axis=1).astype(BF16)
        source = given[slot].astype(F32) + dot(traces, sides).T
        placed[slot] = dot(inverse[slot], source.astype(BF16)).astype(BF16)


def gather_list(value, axis):
    values = [value]
    for mask in bits_of(lax.axis_size(axis))[::-1]:
        values = values + [swap(v, axis, mask) for v in values]
    return values


def exchange(value, axis):
    groups = value.shape[0]
    bits = bits_of(groups)
    rest = value.shape[1:]
    value = value.reshape((2,) * len(bits) + rest)
    for dim, mask in enumerate(bits[::-1]):
        kept = lax.index_in_dim(value, 0, dim, keepdims=True)
        sent = lax.index_in_dim(value, 1, dim, keepdims=True)
        value = jnp.concatenate([kept, swap(sent, axis, mask)], axis=dim)
    return value.reshape((groups,) + rest)


def shards(right_sides, inverse, coupling, sweep_order):
    given = right_sides[0, 0]
    inverse = inverse[0, 0]
    order = sweep_order[0, 0]
    count, nodes, width = given.shape
    face = coupling.shape[4]
    coupling = coupling[0, 0].reshape(count, 3 * face, nodes)
    groups = lax.axis_size("span")
    share = width // groups
    half = groups // 2
    me = lax.axis_index("span")
    place = me.astype(jnp.int32).reshape(1)
    line = lax.axis_index("stream").astype(jnp.int32)
    masks = bits_of(lax.axis_size("stream"))
    flags = jnp.stack([(line // mask) % 2 for mask in masks])
    map_rows = (count + count // 2) * 3 * face
    maps, gains = pl.pallas_call(
        functools.partial(facemap_kernel, groups=groups),
        out_shape=(
            jax.ShapeDtypeStruct((map_rows, 2 * face), BF16),
            jax.ShapeDtypeStruct((groups, count, share, 4 * face), BF16),
        ),
        in_specs=[SMEM, SMEM, VMEM, VMEM, VMEM],
        out_specs=(VMEM, VMEM),
        name="facemaps",
    )(place, order, inverse, coupling, given)
    all_maps = gather_list(maps, "span")
    gains = exchange(gains, "span")
    rows = share + half * face
    response, offset = pl.pallas_call(
        functools.partial(respond_kernel, groups=groups, count=count, face=face),
        out_shape=(
            jax.ShapeDtypeStruct((SWEEPS, half * face, half * face), BF16),
            jax.ShapeDtypeStruct((SWEEPS, share, groups * face), BF16),
        ),
        in_specs=[SMEM] + [VMEM] * (groups + 1),
        out_specs=(VMEM, VMEM),
        scratch_shapes=[
            pltpu.VMEM((groups, count, 4 * face, 4 * face), BF16),
            pltpu.VMEM((2, groups + 1, count, rows, 2 * face), BF16),
            pltpu.VMEM((2, groups, rows, 2 * face), BF16),
        ],
        name="respond",
    )(place, *all_maps, gains)
    levels = []
    for level, mask in enumerate(masks[:-1]):
        other = swap(response, "span", 1)
        got = swap(response, "stream", mask)
        got_offset = swap(offset, "stream", mask)
        got_other = swap(got, "span", 1)
        levels += [got, got_other, got_offset]
        response, offset = pl.pallas_call(
            compose_kernel,
            out_shape=(
                jax.ShapeDtypeStruct(response.shape, BF16),
                jax.ShapeDtypeStruct(offset.shape, BF16),
            ),
            in_specs=[SMEM] + [VMEM] * 6,
            out_specs=(VMEM, VMEM),
            name="compose",
        )(flags[level : level + 1], response, other, got, got_other, offset, got_offset)
    top = swap(offset, "stream", masks[-1])
    wanted = pl.pallas_call(
        functools.partial(
            resolve_kernel, groups=groups, count=count, face=face, levels=len(masks) - 1
        ),
        out_shape=jax.ShapeDtypeStruct((groups, count + count // 2, share, 2 * face), BF16),
        in_specs=[SMEM, SMEM] + [VMEM] * (groups + 2 + len(levels)),
        out_specs=VMEM,
        scratch_shapes=[
            pltpu.VMEM((groups, count, 4 * face, 4 * face), BF16),
            pltpu.VMEM((2, groups + 1, count, share, 2 * face), BF16),
            pltpu.VMEM((SWEEPS, groups, share, 2 * face), BF16),
        ],
        name="resolve",
    )(place, flags, *all_maps, gains, top, *levels)
    wanted = exchange(wanted, "span")
    placed = pl.pallas_call(
        functools.partial(final_kernel, groups=groups),
        out_shape=jax.ShapeDtypeStruct((count, nodes, width), BF16),
        in_specs=[SMEM, SMEM] + [VMEM] * 4,
        out_specs=VMEM,
        scratch_shapes=[pltpu.VMEM((count + count // 2, width, 2 * face), F32)],
        name="finish",
    )(place, order, inverse, coupling, given, wanted)
    return placed[None, None]


def solution(mesh):
    in_specs = (
        P("stream", "span", None, None, None),
        P("stream", "span", None, None, None),
        P("stream", "span", None, None, None, None),
        P("stream", "span", None),
    )
    out_specs = P("stream", "span", None, None, None)
    return jax.shard_map(shards, mesh=mesh, in_specs=in_specs, out_specs=out_specs, check_vma=False)
```

time: 419 us -> 105 us (0.25); the launches traced: 414 us -> 104 us
  blocking collectives: 222 us -> 0 us
  matrix products: 159 us -> 0 us
  Pallas kernels: 0 us -> 46.1 us
  waiting for transfers between devices: 0.03 us -> 36.6 us
  between operations: 8.32 us -> 0.13 us
  starting transfers between devices: 21.9 us -> 14.7 us
    all_gather x7 -> x0, blocking collectives: 222 us -> none  [prefix_2(): lax.all_gather(a.astype(kind), axis)]
    dot_general x113 -> x0, matrix products: 159 us -> none  [the longest x65 70.7 us: exact_dot(): jnp.dot(left, right, precision=lax.Precision.HIGHEST, preferred_element_t...]
    pallas_call x0 -> x6, Pallas kernels: none -> 46.1 us  [the longest x1 18 us: shards(): pl.pallas_call(functools.partial(respond_kernel, groups=groups, count=cou...]
    ppermute x10 -> x16, waiting for transfers between devices: 0.03 us -> 36.6 us  [swap(): return lax.ppermute(value, axis, [(i, i ^ mask) for i in range(count)])]
    ppermute x10 -> x16, starting transfers between devices: 21.9 us -> 14.7 us  [swap(): return lax.ppermute(value, axis, [(i, i ^ mask) for i in range(count)])]
  transfers between devices with their start and end apart: 10 -> 16, of which waited for: 0 -> 10; matrix products, arithmetic and copies ran while one was open for 4% -> 2% of each run, Pallas kernels for 0% -> 0%
where the time goes in v1:
time: 105 us; the launch traced here: 104 us
  Pallas kernels  46.1 us (44%)
  waiting for transfers between devices  36.6 us (35%)
  starting transfers between devices  14.7 us (14%)
  local copies, waits for them, and re-layouts  4.91 us (5%)
  other arithmetic  2.09 us (2%)
    ppermute x16, waiting for transfers between devices, swap(): return lax.ppermute(value, axis, [(i, i ^ mask) for i in range(count)])  36.6 us
    pallas_call x1, Pallas kernels, shards(): pl.pallas_call(functools.partial(respond_kernel, groups=groups, count=cou...  18 us
    pallas_call x1, Pallas kernels, shards(): pl.pallas_call(functools.partial(resolve_kernel, groups=groups, count=cou...  15.5 us
    ppermute x16, starting transfers between devices, swap(): return lax.ppermute(value, axis, [(i, i ^ mask) for i in range(count)])  14.7 us
    pallas_call x2, Pallas kernels, shards(): pl.pallas_call(compose_kernel, out_shape=(jax.ShapeDtypeStruct(response.s...  5.21 us
    pallas_call x1, Pallas kernels, shards(): pl.pallas_call(functools.partial(final_kernel, groups=groups), out_shape=...  4.02 us
    pallas_call x1, Pallas kernels, shards(): pl.pallas_call(functools.partial(facemap_kernel, groups=groups), out_shap...  3.37 us
    unnamed x24, local copies, waits for them, and re-layouts  2.97 us
  transfers between devices with their start and end apart: 16, of which 10 were waited for; matrix products, arithmetic and copies ran while one was open for 2% of the time, Pallas kernels for 0%

profile of v1, /device:TPU:0, one launch (start us, length us, event | category | flops | bytes accessed | tf_op | source)
XLA Modules:
  0.0 104.5 jit_solution(13196887838288544239)
XLA Ops:
  0.0 3.4 %facemaps.1 = (bf16[1152,128]{1,0:T(8,128)(2,1)}, bf16[4,4,32,256]{3,2,1,0:T(8,128)(2,1)}) custom-call(s32[1]{0:T(128)} %bitcast.place, s32[4]{0:T(128)} %bitcast.28, bf16[4,512,512]{2,1,0:T(8,128)(2,1)} %bitcast.19, bf16[4,192,512]{2,1,0:T(8,128)(2,1)} %bitcast.21, bf16[4,512,128]{2,1,0:T(8,128)(2,1)} %bitcast.25), custom_call_target="tpu_custom_call" | custom-call | tf_op jit(solution)/shard_map/facemaps/pallas_call | solution.py:329
  3.4 3.0 %collective-permute-start = (bf16[1152,128]{1,0:T(8,128)(2,1)}, bf16[1152,128]{1,0:T(8,128)(2,1)S(1)}, u32[]{:S(2)}, u32[]{:S(2)}) collective-permute-start(bf16[1152,128]{1,0:T(8,128)(2,1)} %get-tuple-element.12.refs_0_), channel_id=1, source_target_pairs={{0,2},{1,3},{2,0},{3,1},{4,6},{5,7},{6,4},{7,5},{8,10},{9,11},{10,... | collective-permute-start | bytes 884744 | tf_op jit(solution)/shard_map/ppermute | solution.py:37
  6.3 1.0 slice_bitcast_fusion.1
  7.5 6.9 %collective-permute-done.refs_1_ = bf16[1152,128]{1,0:T(8,128)(2,1)S(1)} collective-permute-done((bf16[1152,128]{1,0:T(8,128)(2,1)}, bf16[1152,128]{1,0:T(8,128)(2,1)S(1)}, u32[]{:S(2)}, u32[]{:S(2)}) %collective-permute-start) | collective-permute-done | bytes 294944 | tf_op jit(solution)/shard_map/ppermute | solution.py:37
  14.4 1.9 %collective-permute-done.3 = bf16[1,2,4,32,256]{4,3,2,1,0:T(8,128)(2,1)S(1)} collective-permute-done((bf16[1,2,4,32,256]{4,3,2,1,0:T(8,128)(2,1)S(1)}, bf16[1,2,4,32,256]{4,3,2,1,0:T(8,128)(2,1)S(1)}, u32[]{:S(2)}, u32[]{:S(2)}) %collective-permute-start.3) | collective-permute-done | bytes 131104 | tf_op jit(solution)/shard_map/ppermute | solution.py:37
  16.5 1.3 %collective-permute-done.4 = bf16[2,1,4,32,256]{4,3,2,1,0:T(8,128)(2,1)S(1)} collective-permute-done((bf16[2,1,4,32,256]{4,3,2,1,0:T(8,128)(2,1)S(1)}, bf16[2,1,4,32,256]{4,3,2,1,0:T(8,128)(2,1)S(1)}, u32[]{:S(2)}, u32[]{:S(2)}) %collective-permute-start.4) | collective-permute-done | bytes 131104 | tf_op jit(solution)/shard_map/ppermute | solution.py:37
  19.3 18.0 %respond.1 = (bf16[6,128,128]{2,1,0:T(8,128)(2,1)}, bf16[6,32,256]{2,1,0:T(8,128)(2,1)}) custom-call(s32[1]{0:T(128)} %bitcast.place, bf16[1152,128]{1,0:T(8,128)(2,1)} %get-tuple-element.12.refs_0_, bf16[1152,128]{1,0:T(8,128)(2,1)} %copy-done, bf16[1152,128]{1,0:T(8,128)(2,1)} %copy-done.1, bf16[1152,128]{1,0:T(8,128)(2,1)} %copy-done.2, ...), custom_call_target="tpu_custom_call" | custom-call | tf_op jit(solution)/shard_map/respond/pallas_call | solution.py:342
  37.3 1.8 %collective-permute-start.6 = (bf16[6,128,128]{2,1,0:T(8,128)(2,1)}, bf16[6,128,128]{2,1,0:T(8,128)(2,1)S(1)}, u32[]{:S(2)}, u32[]{:S(2)}) collective-permute-start(bf16[6,128,128]{2,1,0:T(8,128)(2,1)} %get-tuple-element.14.own_even), channel_id=1, source_target_pairs={{0,4},{4,0},{8,12},{12,8},{16,20},{20,16},{24,28},{28,24},{1,5},{5... | collective-permute-start | bytes 589832 | tf_op jit(solution)/shard_map/ppermute | solution.py:37
  39.1 5.4 %collective-permute-done.6.got_even.refs_6_ = bf16[6,128,128]{2,1,0:T(8,128)(2,1)S(1)} collective-permute-done((bf16[6,128,128]{2,1,0:T(8,128)(2,1)}, bf16[6,128,128]{2,1,0:T(8,128)(2,1)S(1)}, u32[]{:S(2)}, u32[]{:S(2)}) %collective-permute-start.6) | collective-permute-done | bytes 196640 | tf_op jit(solution)/shard_map/ppermute | solution.py:37
  44.5 1.7 %collective-permute-start.8 = (bf16[6,32,256]{2,1,0:T(8,128)(2,1)}, bf16[6,32,256]{2,1,0:T(8,128)(2,1)S(1)}, u32[]{:S(2)}, u32[]{:S(2)}) collective-permute-start(bf16[6,32,256]{2,1,0:T(8,128)(2,1)} %get-tuple-element.15.own_offset), channel_id=1, source_target_pairs={{0,4},{4,0},{8,12},{12,8},{16,20},{20,16},{24,28},{28,24},{1,5},{5... | collective-permute-start | bytes 294920 | tf_op jit(solution)/shard_map/ppermute | solution.py:37
  46.3 3.7 %collective-permute-done.8.got_offset.refs_8_ = bf16[6,32,256]{2,1,0:T(8,128)(2,1)S(1)} collective-permute-done((bf16[6,32,256]{2,1,0:T(8,128)(2,1)}, bf16[6,32,256]{2,1,0:T(8,128)(2,1)S(1)}, u32[]{:S(2)}, u32[]{:S(2)}) %collective-permute-start.8) | collective-permute-done | bytes 98336 | tf_op jit(solution)/shard_map/ppermute | solution.py:37
  50.8 2.6 %compose.2 = (bf16[6,128,128]{2,1,0:T(8,128)(2,1)}, bf16[6,32,256]{2,1,0:T(8,128)(2,1)}) custom-call(s32[1]{0:T(128)} %bitcast.5.flag, bf16[6,128,128]{2,1,0:T(8,128)(2,1)} %get-tuple-element.14.own_even, bf16[6,128,128]{2,1,0:T(8,128)(2,1)} %copy-done.10, bf16[6,128,128]{2,1,0:T(8,128)(2,1)} %copy-done.3, bf16[6,128,128]{2,1,0:T(8,128)(2,1)} %copy-done.4, ...), custom_call_target="tpu_custom_call" | custom-call | tf_op jit(solution)/shard_map/compose/pallas_call | solution.py:364
  53.4 1.8 %collective-permute-start.10 = (bf16[6,128,128]{2,1,0:T(8,128)(2,1)}, bf16[6,128,128]{2,1,0:T(8,128)(2,1)S(1)}, u32[]{:S(2)}, u32[]{:S(2)}) collective-permute-start(bf16[6,128,128]{2,1,0:T(8,128)(2,1)} %get-tuple-element.16.own_even), channel_id=1, source_target_pairs={{0,8},{4,12},{8,0},{12,4},{16,24},{20,28},{24,16},{28,20},{1,9},{5... | collective-permute-start | bytes 589832 | tf_op jit(solution)/shard_map/ppermute | solution.py:37
  55.1 4.9 %collective-permute-done.10.got_even.refs_9_ = bf16[6,128,128]{2,1,0:T(8,128)(2,1)S(1)} collective-permute-done((bf16[6,128,128]{2,1,0:T(8,128)(2,1)}, bf16[6,128,128]{2,1,0:T(8,128)(2,1)S(1)}, u32[]{:S(2)}, u32[]{:S(2)}) %collective-permute-start.10) | collective-permute-done | bytes 196640 | tf_op jit(solution)/shard_map/ppermute | solution.py:37
  60.1 1.7 %collective-permute-start.12 = (bf16[6,32,256]{2,1,0:T(8,128)(2,1)}, bf16[6,32,256]{2,1,0:T(8,128)(2,1)S(1)}, u32[]{:S(2)}, u32[]{:S(2)}) collective-permute-start(bf16[6,32,256]{2,1,0:T(8,128)(2,1)} %get-tuple-element.17.own_offset), channel_id=1, source_target_pairs={{0,8},{4,12},{8,0},{12,4},{16,24},{20,28},{24,16},{28,20},{1,9},{5... | collective-permute-start | bytes 294920 | tf_op jit(solution)/shard_map/ppermute | solution.py:37
  61.8 3.7 %collective-permute-done.12.got_offset.refs_11_ = bf16[6,32,256]{2,1,0:T(8,128)(2,1)S(1)} collective-permute-done((bf16[6,32,256]{2,1,0:T(8,128)(2,1)}, bf16[6,32,256]{2,1,0:T(8,128)(2,1)S(1)}, u32[]{:S(2)}, u32[]{:S(2)}) %collective-permute-start.12) | collective-permute-done | bytes 98336 | tf_op jit(solution)/shard_map/ppermute | solution.py:37
  66.3 2.6 %compose.3 = (bf16[6,128,128]{2,1,0:T(8,128)(2,1)}, bf16[6,32,256]{2,1,0:T(8,128)(2,1)}) custom-call(s32[1]{0:T(128)} %bitcast.6.flag, bf16[6,128,128]{2,1,0:T(8,128)(2,1)} %get-tuple-element.16.own_even, bf16[6,128,128]{2,1,0:T(8,128)(2,1)} %copy-done.9, bf16[6,128,128]{2,1,0:T(8,128)(2,1)} %copy-done.5, bf16[6,128,128]{2,1,0:T(8,128)(2,1)} %copy-done.6, ...), custom_call_target="tpu_custom_call" | custom-call | tf_op jit(solution)/shard_map/compose/pallas_call | solution.py:364
  68.9 2.7 %collective-permute-start.13 = (bf16[6,32,256]{2,1,0:T(8,128)(2,1)}, bf16[6,32,256]{2,1,0:T(8,128)(2,1)S(1)}, u32[]{:S(2)}, u32[]{:S(2)}) collective-permute-start(bf16[6,32,256]{2,1,0:T(8,128)(2,1)} %get-tuple-element.18), channel_id=1, source_target_pairs={{0,16},{4,20},{8,24},{12,28},{16,0},{20,4},{24,8},{28,12},{1,17},{... | collective-permute-start | bytes 294920 | tf_op jit(solution)/shard_map/ppermute | solution.py:37
  72.3 4.3 %collective-permute-done.13.refs_5_ = bf16[6,32,256]{2,1,0:T(8,128)(2,1)S(1)} collective-permute-done((bf16[6,32,256]{2,1,0:T(8,128)(2,1)}, bf16[6,32,256]{2,1,0:T(8,128)(2,1)S(1)}, u32[]{:S(2)}, u32[]{:S(2)}) %collective-permute-start.13) | collective-permute-done | bytes 98336 | tf_op jit(solution)/shard_map/ppermute | solution.py:37
  77.2 15.5 %resolve.1 = bf16[4,6,32,128]{3,2,1,0:T(8,128)(2,1)} custom-call(s32[1]{0:T(128)} %bitcast.place, s32[3]{0:T(128)} %pad_add_fusion.flags, bf16[1152,128]{1,0:T(8,128)(2,1)} %get-tuple-element.12.refs_0_, bf16[1152,128]{1,0:T(8,128)(2,1)} %copy-done, bf16[1152,128]{1,0:T(8,128)(2,1)} %copy-done.1, bf16[1152,128]{1,0:T(8,128)(2,1)} %copy-done.2, ...), custom_call_target="tpu_custom_call" | custom-call | tf_op jit(solution)/shard_map/resolve/pallas_call | solution.py:375
  93.7 1.6 %collective-permute-start.14 = (bf16[1,2,6,32,128]{4,3,2,1,0:T(8,128)(2,1)S(1)}, bf16[1,2,6,32,128]{4,3,2,1,0:T(8,128)(2,1)S(1)}, u32[]{:S(2)}, u32[]{:S(2)}) collective-permute-start(bf16[1,2,6,32,128]{4,3,2,1,0:T(8,128)(2,1)S(1)} %get-tuple-element.26), channel_id=1, source_target_pairs={{0,2},{1,3},{2,0},{3,1},{4,6},{5,7},{6,4},{7,5},{8,10},{9,11},{10,... | collective-permute-start | bytes 294920 | tf_op jit(solution)/shard_map/ppermute | solution.py:37
  95.3 3.1 %collective-permute-done.14 = bf16[1,2,6,32,128]{4,3,2,1,0:T(8,128)(2,1)S(1)} collective-permute-done((bf16[1,2,6,32,128]{4,3,2,1,0:T(8,128)(2,1)S(1)}, bf16[1,2,6,32,128]{4,3,2,1,0:T(8,128)(2,1)S(1)}, u32[]{:S(2)}, u32[]{:S(2)}) %collective-permute-start.14) | collective-permute-done | bytes 98336 | tf_op jit(solution)/shard_map/ppermute | solution.py:37
  98.5 1.3 %collective-permute-done.15 = bf16[2,1,6,32,128]{4,3,2,1,0:T(8,128)(2,1)S(1)} collective-permute-done((bf16[2,1,6,32,128]{4,3,2,1,0:T(8,128)(2,1)S(1)}, bf16[2,1,6,32,128]{4,3,2,1,0:T(8,128)(2,1)S(1)}, u32[]{:S(2)}, u32[]{:S(2)}) %collective-permute-start.15) | collective-permute-done | bytes 98336 | tf_op jit(solution)/shard_map/ppermute | solution.py:37
  100.5 4.0 %finish.1 = bf16[4,512,128]{2,1,0:T(8,128)(2,1)} custom-call(s32[1]{0:T(128)} %bitcast.place, s32[4]{0:T(128)} %bitcast.29, bf16[4,512,512]{2,1,0:T(8,128)(2,1)} %bitcast.20, bf16[4,192,512]{2,1,0:T(8,128)(2,1)} %bitcast.22, bf16[4,512,128]{2,1,0:T(8,128)(2,1)} %bitcast.26, bf16[4,6,32,128]{3,2,1,0:T(8,128)(2,1)} %bitcast.27), custom_call_target="tpu_custom_call" | custom-call | tf_op jit(solution)/shard_map/finish/pallas_call | solution.py:390
  (45 shorter events, 6.3 us)
Async XLA Ops:
  3.4 11.0 %collective-permute-start = (bf16[1152,128]{1,0:T(8,128)(2,1)}, bf16[1152,128]{1,0:T(8,128)(2,1)S(1)}, u32[]{:S(2)}, u32[]{:S(2)}) collective-permute-start(bf16[1152,128]{1,0:T(8,128)(2,1)} %get-tuple-element.12.refs_0_), channel_id=1, source_target_pairs={{0,2},{1,3},{2,0},{3,1},{4,6},{5,7},{6,4},{7,5},{8,10},{9,11},{10,... | collective-permute-start | bytes 884744 | tf_op jit(solution)/shard_map/ppermute | solution.py:37
  7.3 9.0 %collective-permute-start.3 = (bf16[1,2,4,32,256]{4,3,2,1,0:T(8,128)(2,1)S(1)}, bf16[1,2,4,32,256]{4,3,2,1,0:T(8,128)(2,1)S(1)}, u32[]{:S(2)}, u32[]{:S(2)}) collective-permute-start(bf16[1,2,4,32,256]{4,3,2,1,0:T(8,128)(2,1)S(1)} %get-tuple-element.22), channel_id=1, source_target_pairs={{0,2},{1,3},{2,0},{3,1},{4,6},{5,7},{6,4},{7,5},{8,10},{9,11},{10,... | collective-permute-start | bytes 393224 | tf_op jit(solution)/shard_map/ppermute | solution.py:37
  7.4 11.1 %collective-permute-start.1 = (bf16[1152,128]{1,0:T(8,128)(2,1)}, bf16[1152,128]{1,0:T(8,128)(2,1)S(1)}, u32[]{:S(2)}, u32[]{:S(2)}) collective-permute-start(bf16[1152,128]{1,0:T(8,128)(2,1)} %get-tuple-element.12.refs_0_), channel_id=1, source_target_pairs={{0,1},{1,0},{2,3},{3,2},{4,5},{5,4},{6,7},{7,6},{8,9},{9,8},{10,11... | collective-permute-start | bytes 884744 | tf_op jit(solution)/shard_map/ppermute | solution.py:37
  14.4 4.1 %copy-start = (bf16[1152,128]{1,0:T(8,128)(2,1)}, bf16[1152,128]{1,0:T(8,128)(2,1)S(1)}, u32[]{:S(2)}) copy-start(bf16[1152,128]{1,0:T(8,128)(2,1)S(1)} %collective-permute-done.refs_1_) | copy-start | bytes 884740
  14.4 4.1 %collective-permute-start.2 = (bf16[1152,128]{1,0:T(8,128)(2,1)S(1)}, bf16[1152,128]{1,0:T(8,128)(2,1)S(1)}, u32[]{:S(2)}, u32[]{:S(2)}) collective-permute-start(bf16[1152,128]{1,0:T(8,128)(2,1)S(1)} %collective-permute-done.refs_1_), channel_id=1, source_target_pairs={{0,1},{1,0},{2,3},{3,2},{4,5},{5,4},{6,7},{7,6},{8,9},{9,8},{10,11... | collective-permute-start | bytes 884744 | tf_op jit(solution)/shard_map/ppermute | solution.py:37
  16.4 1.4 %collective-permute-start.4 = (bf16[2,1,4,32,256]{4,3,2,1,0:T(8,128)(2,1)S(1)}, bf16[2,1,4,32,256]{4,3,2,1,0:T(8,128)(2,1)S(1)}, u32[]{:S(2)}, u32[]{:S(2)}) collective-permute-start(bf16[2,1,4,32,256]{4,3,2,1,0:T(8,128)(2,1)S(1)} %get-tuple-element.20), channel_id=1, source_target_pairs={{0,1},{1,0},{2,3},{3,2},{4,5},{5,4},{6,7},{7,6},{8,9},{9,8},{10,11... | collective-permute-start | bytes 393224 | tf_op jit(solution)/shard_map/ppermute | solution.py:37
  18.5 0.8 copy-start.2
  37.3 7.2 %collective-permute-start.6 = (bf16[6,128,128]{2,1,0:T(8,128)(2,1)}, bf16[6,128,128]{2,1,0:T(8,128)(2,1)S(1)}, u32[]{:S(2)}, u32[]{:S(2)}) collective-permute-start(bf16[6,128,128]{2,1,0:T(8,128)(2,1)} %get-tuple-element.14.own_even), channel_id=1, source_target_pairs={{0,4},{4,0},{8,12},{12,8},{16,20},{20,16},{24,28},{28,24},{1,5},{5... | collective-permute-start | bytes 589832 | tf_op jit(solution)/shard_map/ppermute | solution.py:37
  39.1 10.9 %collective-permute-start.5 = (bf16[6,128,128]{2,1,0:T(8,128)(2,1)}, bf16[6,128,128]{2,1,0:T(8,128)(2,1)S(1)}, u32[]{:S(2)}, u32[]{:S(2)}) collective-permute-start(bf16[6,128,128]{2,1,0:T(8,128)(2,1)} %get-tuple-element.14.own_even), channel_id=1, source_target_pairs={{0,1},{1,0},{2,3},{3,2},{4,5},{5,4},{6,7},{7,6},{8,9},{9,8},{10,11... | collective-permute-start | bytes 589832 | tf_op jit(solution)/shard_map/ppermute | solution.py:37
  44.5 5.4 %copy-start.3 = (bf16[6,128,128]{2,1,0:T(8,128)(2,1)}, bf16[6,128,128]{2,1,0:T(8,128)(2,1)S(1)}, u32[]{:S(2)}) copy-start(bf16[6,128,128]{2,1,0:T(8,128)(2,1)S(1)} %collective-permute-done.6.got_even.refs_6_) | copy-start | bytes 589828
  44.5 5.4 %collective-permute-start.7 = (bf16[6,128,128]{2,1,0:T(8,128)(2,1)S(1)}, bf16[6,128,128]{2,1,0:T(8,128)(2,1)S(1)}, u32[]{:S(2)}, u32[]{:S(2)}) collective-permute-start(bf16[6,128,128]{2,1,0:T(8,128)(2,1)S(1)} %collective-permute-done.6.got_even.refs_6_), channel_id=1, source_target_pairs={{0,1},{1,0},{2,3},{3,2},{4,5},{5,4},{6,7},{7,6},{8,9},{9,8},{10,11... | collective-permute-start | bytes 589832 | tf_op jit(solution)/shard_map/ppermute | solution.py:37
  44.5 5.4 %collective-permute-start.8 = (bf16[6,32,256]{2,1,0:T(8,128)(2,1)}, bf16[6,32,256]{2,1,0:T(8,128)(2,1)S(1)}, u32[]{:S(2)}, u32[]{:S(2)}) collective-permute-start(bf16[6,32,256]{2,1,0:T(8,128)(2,1)} %get-tuple-element.15.own_offset), channel_id=1, source_target_pairs={{0,4},{4,0},{8,12},{12,8},{16,20},{20,16},{24,28},{28,24},{1,5},{5... | collective-permute-start | bytes 294920 | tf_op jit(solution)/shard_map/ppermute | solution.py:37
  50.0 0.7 copy-start.10
  50.0 0.8 copy-start.4
  53.4 6.7 %collective-permute-start.10 = (bf16[6,128,128]{2,1,0:T(8,128)(2,1)}, bf16[6,128,128]{2,1,0:T(8,128)(2,1)S(1)}, u32[]{:S(2)}, u32[]{:S(2)}) collective-permute-start(bf16[6,128,128]{2,1,0:T(8,128)(2,1)} %get-tuple-element.16.own_even), channel_id=1, source_target_pairs={{0,8},{4,12},{8,0},{12,4},{16,24},{20,28},{24,16},{28,20},{1,9},{5... | collective-permute-start | bytes 589832 | tf_op jit(solution)/shard_map/ppermute | solution.py:37
  55.1 10.3 %collective-permute-start.9 = (bf16[6,128,128]{2,1,0:T(8,128)(2,1)}, bf16[6,128,128]{2,1,0:T(8,128)(2,1)S(1)}, u32[]{:S(2)}, u32[]{:S(2)}) collective-permute-start(bf16[6,128,128]{2,1,0:T(8,128)(2,1)} %get-tuple-element.16.own_even), channel_id=1, source_target_pairs={{0,1},{1,0},{2,3},{3,2},{4,5},{5,4},{6,7},{7,6},{8,9},{9,8},{10,11... | collective-permute-start | bytes 589832 | tf_op jit(solution)/shard_map/ppermute | solution.py:37
  60.1 5.4 %copy-start.5 = (bf16[6,128,128]{2,1,0:T(8,128)(2,1)}, bf16[6,128,128]{2,1,0:T(8,128)(2,1)S(1)}, u32[]{:S(2)}) copy-start(bf16[6,128,128]{2,1,0:T(8,128)(2,1)S(1)} %collective-permute-done.10.got_even.refs_9_) | copy-start | bytes 589828
  60.1 5.4 %collective-permute-start.11 = (bf16[6,128,128]{2,1,0:T(8,128)(2,1)S(1)}, bf16[6,128,128]{2,1,0:T(8,128)(2,1)S(1)}, u32[]{:S(2)}, u32[]{:S(2)}) collective-permute-start(bf16[6,128,128]{2,1,0:T(8,128)(2,1)S(1)} %collective-permute-done.10.got_even.refs_9_), channel_id=1, source_target_pairs={{0,1},{1,0},{2,3},{3,2},{4,5},{5,4},{6,7},{7,6},{8,9},{9,8},{10,11... | collective-permute-start | bytes 589832 | tf_op jit(solution)/shard_map/ppermute | solution.py:37
  60.1 5.4 %collective-permute-start.12 = (bf16[6,32,256]{2,1,0:T(8,128)(2,1)}, bf16[6,32,256]{2,1,0:T(8,128)(2,1)S(1)}, u32[]{:S(2)}, u32[]{:S(2)}) collective-permute-start(bf16[6,32,256]{2,1,0:T(8,128)(2,1)} %get-tuple-element.17.own_offset), channel_id=1, source_target_pairs={{0,8},{4,12},{8,0},{12,4},{16,24},{20,28},{24,16},{28,20},{1,9},{5... | collective-permute-start | bytes 294920 | tf_op jit(solution)/shard_map/ppermute | solution.py:37
  65.5 0.7 copy-start.9
  65.5 0.8 copy-start.6
  68.9 7.7 %collective-permute-start.13 = (bf16[6,32,256]{2,1,0:T(8,128)(2,1)}, bf16[6,32,256]{2,1,0:T(8,128)(2,1)S(1)}, u32[]{:S(2)}, u32[]{:S(2)}) collective-permute-start(bf16[6,32,256]{2,1,0:T(8,128)(2,1)} %get-tuple-element.18), channel_id=1, source_target_pairs={{0,16},{4,20},{8,24},{12,28},{16,0},{20,4},{24,8},{28,12},{1,17},{... | collective-permute-start | bytes 294920 | tf_op jit(solution)/shard_map/ppermute | solution.py:37
  93.7 4.7 %collective-permute-start.14 = (bf16[1,2,6,32,128]{4,3,2,1,0:T(8,128)(2,1)S(1)}, bf16[1,2,6,32,128]{4,3,2,1,0:T(8,128)(2,1)S(1)}, u32[]{:S(2)}, u32[]{:S(2)}) collective-permute-start(bf16[1,2,6,32,128]{4,3,2,1,0:T(8,128)(2,1)S(1)} %get-tuple-element.26), channel_id=1, source_target_pairs={{0,2},{1,3},{2,0},{3,1},{4,6},{5,7},{6,4},{7,5},{8,10},{9,11},{10,... | collective-permute-start | bytes 294920 | tf_op jit(solution)/shard_map/ppermute | solution.py:37
  98.4 1.4 %collective-permute-start.15 = (bf16[2,1,6,32,128]{4,3,2,1,0:T(8,128)(2,1)S(1)}, bf16[2,1,6,32,128]{4,3,2,1,0:T(8,128)(2,1)S(1)}, u32[]{:S(2)}, u32[]{:S(2)}) collective-permute-start(bf16[2,1,6,32,128]{4,3,2,1,0:T(8,128)(2,1)S(1)} %get-tuple-element.24), channel_id=1, source_target_pairs={{0,1},{1,0},{2,3},{3,2},{4,5},{5,4},{6,7},{7,6},{8,9},{9,8},{10,11... | collective-permute-start | bytes 294920 | tf_op jit(solution)/shard_map/ppermute | solution.py:37
  (4 other events, 2.6 us)

commit v2 on v1

v2 whole, which is shorter than its diff:
```python
import functools

import jax
import jax.numpy as jnp
from jax import lax
from jax.experimental import pallas as pl
from jax.experimental.pallas import tpu as pltpu
from jax.sharding import PartitionSpec as P

NP = 8
SWEEPS = 6
VMEM = pl.BlockSpec(memory_space=pltpu.VMEM)
SMEM = pl.BlockSpec(memory_space=pltpu.SMEM)
F32 = jnp.float32
BF16 = jnp.bfloat16


def bits_of(count):
    return [1 << i for i in range(count.bit_length() - 1)]


def reversed_bits(value, count):
    bits = bits_of(count)
    total = 0
    for low, high in zip(bits, bits[::-1]):
        total = total + jnp.where((value & low) != 0, high, 0)
    return total


def reversed_static(value, count):
    bits = bits_of(count)
    return sum(high for low, high in zip(bits, bits[::-1]) if value & low)


def swap(value, axis, mask):
    count = lax.axis_size(axis)
    return lax.ppermute(value, axis, [(i, i ^ mask) for i in range(count)])


def dot(left, right):
    return jnp.dot(left, right, preferred_element_type=F32)


def dot_nt(left, right):
    return lax.dot_general(left, right, (((1,), (1,)), ((), ())), preferred_element_type=F32)


def by_half(low, high):
    lane = lax.broadcasted_iota(jnp.int32, low.shape, low.ndim - 1)
    return jnp.where(lane < low.shape[-1] // 2, low, high)


def turned(value):
    return pltpu.roll(value.astype(F32), value.shape[-1] // 2, 1).astype(value.dtype)


def facemap_kernel(place, order, inverse, coupling, given, maps, *gains):
    groups = len(gains)
    count, nodes, width = given.shape
    face = coupling.shape[1] // 3
    part = nodes // NP
    layer = part // NP
    share = width // groups
    outs = []
    every = []
    for p in range(count):
        slot = order[p]
        lower = []
        upper = []
        for a in range(NP):
            head = inverse[slot, a * part : a * part + 2 * layer, :].astype(F32)
            tail = inverse[slot, (a + 1) * part - 2 * layer : (a + 1) * part, :].astype(F32)
            lower.append(head[:layer])
            upper.append(tail[layer:])
        faces = jnp.concatenate(lower + upper, axis=0).astype(BF16)
        outflow = inverse[slot, nodes - face :, :]
        rows = jnp.concatenate([faces, outflow, outflow], axis=0)
        full = dot_nt(coupling[slot], rows)
        full = jnp.concatenate([full[2 * face :], full[face : 2 * face], full[:face]], axis=0).astype(BF16)
        maps[p * 3 * face : (p + 1) * 3 * face, :] = full[:, : 2 * face]
        outs.append(full[:, 2 * face :])
        if p % 2 == 1:
            at = (count + p // 2) * 3 * face
            maps[at : at + 3 * face, :] = by_half(outs[p - 1], outs[p])
        every.append(dot(rows, given[slot]).T)
    tiles = [gain[:, : 2 * face] for gain in every]
    for p in range(0, count, 2):
        tiles.append(by_half(every[p][:, 2 * face :], every[p + 1][:, 2 * face :]))
    for m, tile in enumerate(tiles):
        tile = tile.astype(BF16)
        for j in range(groups):
            piece = tile[j * share : (j + 1) * share]
            for rel in range(groups):

                @pl.when((place[0] ^ j) == rel)
                def _():
                    gains[rel][m] = piece


def unpack(map_refs, gain_refs, weights, gains, count, face):
    for pos, ref in enumerate(map_refs):
        for p in range(count):
            sides = ref[p * 3 * face : (p + 1) * 3 * face, :]
            at = (count + p // 2) * 3 * face
            outs = ref[at : at + 3 * face, :]
            other = turned(outs)
            outs = by_half(outs, other) if p % 2 == 0 else by_half(other, outs)
            full = jnp.concatenate([sides, outs], axis=1)
            weights[pos, p, : 3 * face, :] = full
            weights[pos, p, 3 * face :, :] = full[2 * face :]
    for pos in range(len(map_refs)):
        ref = gain_refs[reversed_static(pos, len(map_refs))]
        for p in range(count):
            outs = ref[count + p // 2]
            other = turned(outs)
            outs = by_half(outs, other) if p % 2 == 0 else by_half(other, outs)
            gains[pos, p] = jnp.concatenate([ref[p], outs], axis=1).astype(F32)


def neighbours(me, pos, groups):
    own = me ^ reversed_bits(pos, groups)
    below = jnp.where(own > 0, reversed_bits(((own - 1) & (groups - 1)) ^ me, groups), groups)
    above = jnp.where(own < groups - 1, reversed_bits(((own + 1) & (groups - 1)) ^ me, groups), groups)
    return below, above


def read_lags(me, states, lags, groups, count):
    def read(pos):
        below, above = neighbours(me, pos, groups)
        for p in range(count):
            lags[pos, p] = by_half(states[above, p], states[below, p])

    over(groups, read)


def over(count, body, limit=4):
    if count <= limit:
        for i in range(count):
            body(i)
    else:

        def step(i, carry):
            body(i)
            return carry

        lax.fori_loop(0, count, step, 0)


def split_trace(out):
    high = out.astype(BF16)
    return by_half(high, (out - high.astype(F32)).astype(BF16)), high


def run_chains(chosen, entries, lags, weights, gains, states, count, face):
    share = gains.shape[2]
    outs = [[] for _ in chosen]
    for p in range(count):
        for i, pos in enumerate(chosen):
            result = dot(jnp.concatenate([lags[pos, p], entries[i]], axis=1), weights[pos, p])
            first = result[:share] + gains[pos, p]
            if result.shape[0] == share:
                result = first
            else:
                result = jnp.concatenate([first, result[share:]], axis=0)
            states[pos, p] = result[:, : 2 * face].astype(BF16)
            outs[i].append(result[:, 2 * face :])
        if p < count - 1:
            entries = [split_trace(o[p])[0] for o in outs]
    return outs


def respond_kernel(place, *refs, groups, count, face):
    map_refs = refs[:groups]
    gain_refs = refs[groups : 2 * groups]
    pack, weights, gains, states, lags, unit = refs[2 * groups :]
    me = place[0]
    share = gains.shape[2]
    rows = lags.shape[2]
    half = groups // 2
    unpack(map_refs, gain_refs, weights, gains, count, face)
    states[...] = jnp.zeros_like(states)
    unit[...] = jnp.zeros_like(unit)
    row = lax.broadcasted_iota(jnp.int32, (rows, 2 * face), 0) - share
    lane = lax.broadcasted_iota(jnp.int32, (rows, 2 * face), 1)
    for pos in range(half):
        hit = jnp.logical_and(lane < face, row == lane + pos * face)
        unit[0, pos] = jnp.where(hit, 1.0, 0.0).astype(BF16)

    def sweep(k, carry):
        read_lags(me, states, lags, groups, count)

        def block(t):
            chosen = (2 * t, 2 * t + 1, 2 * t + half, 2 * t + half + 1)
            entries = [unit[jnp.minimum(k, 1), pos] for pos in chosen]
            ends = [outs[-1] for outs in run_chains(chosen, entries, lags, weights, gains, states, count, face)]
            even = by_half(ends[0], ends[1])
            odd = by_half(ends[2], ends[3])
            at = pl.ds(pl.multiple_of(t * 2 * face, 2 * face), 2 * face)
            answered = half * face
            pack[k, :answered, at] = (even[share:] + odd[share:]).astype(BF16)
            pack[k, answered : answered + share, at] = even[:share].astype(BF16)
            pack[k, answered + share :, at] = odd[:share].astype(BF16)

        over(groups // 4, block, 1)
        return carry

    lax.fori_loop(0, SWEEPS, sweep, 0)


def pick(flag, first, second):
    return jnp.where(flag != 0, first, second)


def offsets_of(ref, k):
    width = ref.shape[2]
    share = (ref.shape[1] - width) // 2
    return ref[k, width : width + share], ref[k, width + share :]


def compose_kernel(line, own, own_other, got, got_other, pack, *, mask):
    down = (line[0] // mask) % 2
    width = own.shape[2]
    share = (own.shape[1] - width) // 2
    after = []
    before = []
    inner = []
    for k in range(SWEEPS):
        mine = own[k, :width], own_other[k, :width]
        theirs = got[k, :width], got_other[k, :width]
        after.append([pick(down, a, b) for a, b in zip(mine, theirs)])
        before.append(pick(down, theirs[0], mine[0]))
        inner.append([pick(down, b, a) for a, b in zip(offsets_of(own, k), offsets_of(got, k))])
    for m in range(SWEEPS):
        for target in (m % 2, 1 - m % 2):
            stack = jnp.concatenate([after[d][(target + d) % 2] for d in range(m + 1)], axis=0)
            left = jnp.concatenate([inner[m - d][(target + d) % 2] for d in range(m + 1)], axis=1)
            if target == m % 2:
                top = jnp.concatenate([before[m - d] for d in range(m + 1)], axis=1)
                left = jnp.concatenate([top, left], axis=0)
            total = dot(left, stack)
            if target == m % 2:
                pack[m, :width] = total[:width].astype(BF16)
                total = total[width:]
            added = pick(down, offsets_of(own, m)[target], offsets_of(got, m)[target]).astype(F32)
            at = width + target * share
            pack[m, at : at + share] = (total + added).astype(BF16)


def resolve_kernel(place, line, *refs, groups, count, face, masks):
    weights, gains, top = refs[:3]
    levels = len(masks) - 1
    lower = refs[3 : 3 + 2 * levels]
    wanted = refs[3 + 2 * levels : 3 + 2 * levels + groups]
    states, lags, inflows = refs[3 + 2 * levels + groups :]
    me = place[0]
    half = groups // 2
    states[...] = jnp.zeros_like(states)
    flags = [(line[0] // mask) % 2 for mask in masks]
    values = []
    for k in range(SWEEPS):
        both = offsets_of(top, k)
        values.append([pick(flags[levels], b, jnp.zeros_like(b)) for b in both])
    for level in range(levels - 1, -1, -1):
        even, odd = lower[2 * level : 2 * level + 2]
        width = even.shape[2]
        maps = [(even[k, :width], odd[k, :width]) for k in range(SWEEPS)]
        moved = []
        for k in range(SWEEPS):
            pair = []
            for target in (0, 1):
                stack = jnp.concatenate([maps[d][(target + d) % 2] for d in range(k + 1)], axis=0)
                left = jnp.concatenate([values[k - d][(target + d) % 2] for d in range(k + 1)], axis=1)
                total = dot(left, stack) + offsets_of(even, k)[target].astype(F32)
                pair.append(pick(flags[level], total.astype(BF16), values[k][target]))
            moved.append(pair)
        values = moved
    blank = jnp.zeros((values[0][0].shape[0], 2 * face), BF16)
    for k in range(SWEEPS):
        for pos in range(groups):
            tile = (pos % half) // 2
            both = values[k][pos // half][:, tile * 2 * face : (tile + 1) * 2 * face]
            inflows[k, pos] = by_half(both if pos % 2 == 0 else turned(both), blank)

    def sweep(k, carry):
        read_lags(me, states, lags, groups, count)

        def block(t):
            chosen = tuple(4 * t + i for i in range(4))
            run_chains(
                chosen, [inflows[k, pos] for pos in chosen], lags, weights, gains, states, count, face
            )

        over(groups // 4, block, 1)
        return carry

    lax.fori_loop(0, SWEEPS - 1, sweep, 0)
    read_lags(me, states, lags, groups, count)
    for t in range(groups // 4):
        chosen = tuple(4 * t + i for i in range(4))
        entries = [inflows[SWEEPS - 1, pos] for pos in chosen]
        outs = run_chains(chosen, entries, lags, weights, gains, states, count, face)
        for i, pos in enumerate(chosen):
            target = wanted[reversed_static(pos, groups)]
            traces = [entries[i]] + [o.astype(BF16) for o in outs[i][:-1]]
            for p in range(count):
                target[p] = lags[pos, p]
            target[count] = by_half(traces[0], traces[-1])
            for m in range(1, count // 2):
                target[count + m] = by_half(traces[2 * m - 1], traces[2 * m])


def final_kernel(place, order, inverse, coupling, given, *refs):
    wanted = refs[:-2]
    placed, gathered = refs[-2:]
    count, nodes, width = given.shape
    face = coupling.shape[1] // 3
    share = width // len(wanted)
    for rel, ref in enumerate(wanted):
        at = pl.multiple_of((place[0] ^ rel) * share, share)
        for m in range(ref.shape[0]):
            gathered[m, pl.ds(at, share), :] = ref[m].astype(F32)
    blank = jnp.zeros((face, nodes), BF16)
    for p in range(count):
        slot = order[p]
        rows = coupling[slot]
        second = p == count - 1 or (p > 0 and p % 2 == 0)
        tile = 0 if p == count - 1 else (p + 1) // 2
        pair = [blank, rows[:face]] if second else [rows[:face], blank]
        sides = jnp.concatenate([rows[2 * face :], rows[face : 2 * face]] + pair, axis=0)
        traces = jnp.concatenate([gathered[p], gathered[count + tile]], axis=1).astype(BF16)
        source = given[slot].astype(F32) + dot(traces, sides).T
        placed[slot] = dot(inverse[slot], source.astype(BF16)).astype(BF16)


def gather_list(value, axis):
    values = [value]
    for mask in bits_of(lax.axis_size(axis))[::-1]:
        values = values + [swap(v, axis, mask) for v in values]
    return values


def exchange(values, axis):
    return [v if rel == 0 else swap(v, axis, rel) for rel, v in enumerate(values)]


def call(kernel, name, outs, scratch, scalars, arrays):
    def size(shape, kind):
        total = jnp.dtype(kind).itemsize
        for extent in shape:
            total *= extent
        return total

    held = sum(size(o.shape, o.dtype) for o in outs) + sum(size(a.shape, a.dtype) for a in arrays)
    held += sum(size(shape, kind) for shape, kind in scratch)
    return pl.pallas_call(
        kernel,
        out_shape=outs,
        in_specs=[SMEM] * len(scalars) + [VMEM] * len(arrays),
        out_specs=[VMEM] * len(outs),
        scratch_shapes=[pltpu.VMEM(shape, kind) for shape, kind in scratch],
        compiler_params=pltpu.CompilerParams(vmem_limit_bytes=min(held + (6 << 20), 60 << 20)),
        name=name,
    )(*scalars, *arrays)


def shards(right_sides, inverse, coupling, sweep_order):
    given = right_sides[0, 0]
    inverse = inverse[0, 0]
    order = sweep_order[0, 0]
    count, nodes, width = given.shape
    face = coupling.shape[4]
    coupling = coupling[0, 0].reshape(count, 3 * face, nodes)
    groups = lax.axis_size("span")
    share = width // groups
    half = groups // 2
    place = lax.axis_index("span").astype(jnp.int32).reshape(1)
    line = lax.axis_index("stream").astype(jnp.int32).reshape(1)
    masks = bits_of(lax.axis_size("stream"))
    tiles = count + count // 2
    shape = jax.ShapeDtypeStruct
    maps, *gains = call(
        facemap_kernel,
        "facemaps",
        [shape((tiles * 3 * face, 2 * face), BF16)] + [shape((tiles, share, 2 * face), BF16)] * groups,
        [],
        [place, order],
        [inverse, coupling, given],
    )
    all_maps = gather_list(maps, "span")
    gains = exchange(gains, "span")
    rows = share + half * face
    sizes = dict(groups=groups, count=count, face=face)
    pack, weights, gains = call(
        functools.partial(respond_kernel, **sizes),
        "respond",
        [
            shape((SWEEPS, half * face + 2 * share, half * face), BF16),
            shape((groups, count, 4 * face, 4 * face), BF16),
            shape((groups, count, share, 4 * face), F32),
        ],
        [
            ((groups + 1, count, rows, 2 * face), BF16),
            ((groups, count, rows, 2 * face), BF16),
            ((2, groups, rows, 2 * face), BF16),
        ],
        [place],
        [*all_maps, *gains],
    )
    levels = []
    for mask in masks[:-1]:
        other = swap(pack, "span", 1)
        got = swap(pack, "stream", mask)
        got_other = swap(got, "span", 1)
        levels += [got, got_other]
        (pack,) = call(
            functools.partial(compose_kernel, mask=mask),
            "compose",
            [shape(pack.shape, BF16)],
            [],
            [line],
            [pack, other, got, got_other],
        )
    top = swap(pack, "stream", masks[-1])
    wanted = call(
        functools.partial(resolve_kernel, masks=masks, **sizes),
        "resolve",
        [shape((tiles, share, 2 * face), BF16)] * groups,
        [
            ((groups + 1, count, share, 2 * face), BF16),
            ((groups, count, share, 2 * face), BF16),
            ((SWEEPS, groups, share, 2 * face), BF16),
        ],
        [place, line],
        [weights, gains, top, *levels],
    )
    wanted = exchange(wanted, "span")
    (placed,) = call(
        final_kernel,
        "finish",
        [shape((count, nodes, width), BF16)],
        [((tiles, width, 2 * face), F32)],
        [place, order],
        [inverse, coupling, given, *wanted],
    )
    return placed[None, None]


def solution(mesh):
    in_specs = (
        P("stream", "span", None, None, None),
        P("stream", "span", None, None, None),
        P("stream", "span", None, None, None, None),
        P("stream", "span", None),
    )
    out_specs = P("stream", "span", None, None, None)
    return jax.shard_map(shards, mesh=mesh, in_specs=in_specs, out_specs=out_specs, check_vma=False)
```

time: 105 us -> 79.5 us (0.76)
  Pallas kernels: 46.1 us -> 15.8 us
  waiting for transfers between devices: 36.6 us -> 45.8 us
  other arithmetic: 2.09 us -> 0 us
  starting transfers between devices: 14.7 us -> 13.1 us
    pallas_call x6, Pallas kernels: 46.1 us -> 15.8 us  [call(): pl.pallas_call(kernel, out_shape=outs, in_specs=[SMEM] * len(scalars) + [...]
    ppermute x16, waiting for transfers between devices: 36.6 us -> 45.8 us  [swap(): return lax.ppermute(value, axis, [(i, i ^ mask) for i in range(count)])]
    slice x2 -> x0, local copies, waits for them, and re-layouts: 1.94 us -> none  [exchange(): kept = lax.index_in_dim(value, 0, dim, keepdims=True)]
    ppermute x16, starting transfers between devices: 14.7 us -> 13.1 us  [swap(): return lax.ppermute(value, axis, [(i, i ^ mask) for i in range(count)])]
    unnamed x24 -> x16, local copies, waits for them, and re-layouts: 2.97 us -> 4.44 us
    concatenate x4 -> x0, other arithmetic: 1.45 us -> none  [exchange(): value = jnp.concatenate([kept, swap(sent, axis, mask)], axis=dim)]
  transfers between devices with their start and end apart: 16 -> 16, of which waited for: 10 -> 10; matrix products, arithmetic and copies ran while one was open for 2% -> 0% of each run, Pallas kernels for 0% -> 0%
where the time goes in v2:
time: 79.5 us; the launch traced here: 79.2 us
  waiting for transfers between devices  45.8 us (58%)
  Pallas kernels  15.8 us (20%)
  starting transfers between devices  13.1 us (16%)
  local copies, waits for them, and re-layouts  4.44 us (6%)
    ppermute x16, waiting for transfers between devices, swap(): return lax.ppermute(value, axis, [(i, i ^ mask) for i in range(count)])  45.8 us
    pallas_call x6, Pallas kernels, call(): pl.pallas_call(kernel, out_shape=outs, in_specs=[SMEM] * len(scalars) + [...  15.8 us
    ppermute x16, starting transfers between devices, swap(): return lax.ppermute(value, axis, [(i, i ^ mask) for i in range(count)])  13.1 us
    unnamed x16, local copies, waits for them, and re-layouts  4.44 us
  transfers between devices with their start and end apart: 16, of which 10 were waited for; matrix products, arithmetic and copies ran while one was open for 0% of the time, Pallas kernels for 0%

profile of v2, /device:TPU:0, one launch (start us, length us, event | category | flops | bytes accessed | tf_op | source)
XLA Modules:
  0.0 79.2 jit_solution(4879836529919208587)
XLA Ops:
  0.0 1.6 %copy-done = bf16[1,1,4,512,512]{4,3,2,1,0:T(8,128)(2,1)S(1)} copy-done((bf16[1,1,4,512,512]{4,3,2,1,0:T(8,128)(2,1)S(1)}, bf16[1,1,4,512,512]{4,3,2,1,0:T(8,128)(2,1)}, u32[]{:S(2)}) %copy-start) | copy-done | bytes 2097176
  1.6 1.1 %copy-done.2 = bf16[1,1,4,3,64,512]{5,4,3,2,1,0:T(8,128)(2,1)S(1)} copy-done((bf16[1,1,4,3,64,512]{5,4,3,2,1,0:T(8,128)(2,1)S(1)}, bf16[1,1,4,3,64,512]{5,4,3,2,1,0:T(8,128)(2,1)}, u32[]{:S(2)}) %copy-start.2) | copy-done | bytes 786456
  2.7 1.0 %copy-done.4 = bf16[1,1,4,512,128]{4,3,2,1,0:T(8,128)(2,1)S(1)} copy-done((bf16[1,1,4,512,128]{4,3,2,1,0:T(8,128)(2,1)S(1)}, bf16[1,1,4,512,128]{4,3,2,1,0:T(8,128)(2,1)}, u32[]{:S(2)}) %copy-start.4) | copy-done | bytes 524312
  4.4 2.1 %facemaps.1 = (bf16[1152,128]{1,0:T(8,128)(2,1)S(1)}, bf16[6,32,128]{2,1,0:T(8,128)(2,1)S(1)}, bf16[6,32,128]{2,1,0:T(8,128)(2,1)S(1)}, bf16[6,32,128]{2,1,0:T(8,128)(2,1)S(1)}, bf16[6,32,128]{2,1,0:T(8,128)(2,1)S(1)}) custom-call(s32[1]{0:T(128)} %bitcast.place, s32[4]{0:T(128)S(1)} %bitcast.13, bf16[4,512,512]{2,1,0:T(8,128)(2,1)S(1)} %bitcast.7, ...), custom_call_target="tpu_custom_call" | custom-call | tf_op jit(solution)/shard_map/facemaps/pallas_call | solution.py:355
  6.5 3.0 %collective-permute-start = (bf16[1152,128]{1,0:T(8,128)(2,1)S(1)}, bf16[1152,128]{1,0:T(8,128)(2,1)S(1)}, u32[]{:S(2)}, u32[]{:S(2)}) collective-permute-start(bf16[1152,128]{1,0:T(8,128)(2,1)S(1)} %get-tuple-element.17.refs_0_), channel_id=1, source_target_pairs={{0,2},{1,3},{2,0},{3,1},{4,6},{5,7},{6,4},{7,5},{8,10},{9,11},{10,... | collective-permute-start | bytes 884744 | tf_op jit(solution)/shard_map/ppermute | solution.py:37
  9.5 7.0 %collective-permute-done.refs_1_ = bf16[1152,128]{1,0:T(8,128)(2,1)S(1)} collective-permute-done((bf16[1152,128]{1,0:T(8,128)(2,1)S(1)}, bf16[1152,128]{1,0:T(8,128)(2,1)S(1)}, u32[]{:S(2)}, u32[]{:S(2)}) %collective-permute-start) | collective-permute-done | bytes 294944 | tf_op jit(solution)/shard_map/ppermute | solution.py:37
  17.1 1.7 %collective-permute-start.4 = (bf16[6,32,128]{2,1,0:T(8,128)(2,1)S(1)}, bf16[6,32,128]{2,1,0:T(8,128)(2,1)S(1)}, u32[]{:S(2)}, u32[]{:S(2)}) collective-permute-start(bf16[6,32,128]{2,1,0:T(8,128)(2,1)S(1)} %get-tuple-element.20), channel_id=1, source_target_pairs={{0,2},{1,3},{2,0},{3,1},{4,6},{5,7},{6,4},{7,5},{8,10},{9,11},{10,... | collective-permute-start | bytes 147464 | tf_op jit(solution)/shard_map/ppermute | solution.py:37
  18.8 2.3 %collective-permute-done.4.refs_6_ = bf16[6,32,128]{2,1,0:T(8,128)(2,1)S(1)} collective-permute-done((bf16[6,32,128]{2,1,0:T(8,128)(2,1)S(1)}, bf16[6,32,128]{2,1,0:T(8,128)(2,1)S(1)}, u32[]{:S(2)}, u32[]{:S(2)}) %collective-permute-start.4) | collective-permute-done | bytes 49184 | tf_op jit(solution)/shard_map/ppermute | solution.py:37
  21.1 1.6 %collective-permute-done.5.refs_7_ = bf16[6,32,128]{2,1,0:T(8,128)(2,1)S(1)} collective-permute-done((bf16[6,32,128]{2,1,0:T(8,128)(2,1)S(1)}, bf16[6,32,128]{2,1,0:T(8,128)(2,1)S(1)}, u32[]{:S(2)}, u32[]{:S(2)}) %collective-permute-start.5) | collective-permute-done | bytes 49184 | tf_op jit(solution)/shard_map/ppermute | solution.py:37
  22.7 5.0 %respond.1 = (bf16[6,192,128]{2,1,0:T(8,128)(2,1)S(1)}, bf16[4,4,256,256]{3,2,1,0:T(8,128)(2,1)S(1)}, f32[4,4,32,256]{3,2,1,0:T(8,128)S(1)}) custom-call(s32[1]{0:T(128)} %bitcast.place, bf16[1152,128]{1,0:T(8,128)(2,1)S(1)} %get-tuple-element.17.refs_0_, bf16[1152,128]{1,0:T(8,128)(2,1)S(1)} %collective-permute-done.refs_1_, ...), custom_call_target="tpu_custom_call" | custom-call | tf_op jit(solution)/shard_map/respond/pallas_call | solution.py:355
  27.8 1.6 %collective-permute-start.7 = (bf16[6,192,128]{2,1,0:T(8,128)(2,1)S(1)}, bf16[6,192,128]{2,1,0:T(8,128)(2,1)S(1)}, u32[]{:S(2)}, u32[]{:S(2)}) collective-permute-start(bf16[6,192,128]{2,1,0:T(8,128)(2,1)S(1)} %get-tuple-element.24.own), channel_id=1, source_target_pairs={{0,4},{4,0},{8,12},{12,8},{16,20},{20,16},{24,28},{28,24},{1,5},{5... | collective-permute-start | bytes 884744 | tf_op jit(solution)/shard_map/ppermute | solution.py:37
  29.4 7.4 %collective-permute-done.7.got.refs_3_ = bf16[6,192,128]{2,1,0:T(8,128)(2,1)S(1)} collective-permute-done((bf16[6,192,128]{2,1,0:T(8,128)(2,1)S(1)}, bf16[6,192,128]{2,1,0:T(8,128)(2,1)S(1)}, u32[]{:S(2)}, u32[]{:S(2)}) %collective-permute-start.7) | collective-permute-done | bytes 294944 | tf_op jit(solution)/shard_map/ppermute | solution.py:37
  36.8 1.6 %collective-permute-done.8.got_other.refs_4_ = bf16[6,192,128]{2,1,0:T(8,128)(2,1)S(1)} collective-permute-done((bf16[6,192,128]{2,1,0:T(8,128)(2,1)S(1)}, bf16[6,192,128]{2,1,0:T(8,128)(2,1)S(1)}, u32[]{:S(2)}, u32[]{:S(2)}) %collective-permute-start.8) | collective-permute-done | bytes 294944 | tf_op jit(solution)/shard_map/ppermute | solution.py:37
  38.4 1.5 %compose.2.own = bf16[6,192,128]{2,1,0:T(8,128)(2,1)S(1)} custom-call(s32[1]{0:T(128)} %bitcast.5.line, bf16[6,192,128]{2,1,0:T(8,128)(2,1)S(1)} %get-tuple-element.24.own, bf16[6,192,128]{2,1,0:T(8,128)(2,1)} %collective-permute-done.6.own_other, bf16[6,192,128]{2,1,0:T(8,128)(2,1)S(1)} %collective-permute-done.7.got.refs_3_, ...), custom_call_target="tpu_custom_call" | custom-call | tf_op jit(solution)/shard_map/compose/pallas_call | solution.py:355
  39.8 1.6 %collective-permute-start.10 = (bf16[6,192,128]{2,1,0:T(8,128)(2,1)S(1)}, bf16[6,192,128]{2,1,0:T(8,128)(2,1)S(1)}, u32[]{:S(2)}, u32[]{:S(2)}) collective-permute-start(bf16[6,192,128]{2,1,0:T(8,128)(2,1)S(1)} %compose.2.own), channel_id=1, source_target_pairs={{0,8},{4,12},{8,0},{12,4},{16,24},{20,28},{24,16},{28,20},{1,9},{5... | collective-permute-start | bytes 884744 | tf_op jit(solution)/shard_map/ppermute | solution.py:37
  41.5 7.5 %collective-permute-done.10.got.refs_5_ = bf16[6,192,128]{2,1,0:T(8,128)(2,1)S(1)} collective-permute-done((bf16[6,192,128]{2,1,0:T(8,128)(2,1)S(1)}, bf16[6,192,128]{2,1,0:T(8,128)(2,1)S(1)}, u32[]{:S(2)}, u32[]{:S(2)}) %collective-permute-start.10) | collective-permute-done | bytes 294944 | tf_op jit(solution)/shard_map/ppermute | solution.py:37
  49.0 1.6 %collective-permute-done.11.got_other.refs_6_ = bf16[6,192,128]{2,1,0:T(8,128)(2,1)S(1)} collective-permute-done((bf16[6,192,128]{2,1,0:T(8,128)(2,1)S(1)}, bf16[6,192,128]{2,1,0:T(8,128)(2,1)S(1)}, u32[]{:S(2)}, u32[]{:S(2)}) %collective-permute-start.11) | collective-permute-done | bytes 294944 | tf_op jit(solution)/shard_map/ppermute | solution.py:37
  51.1 2.7 %collective-permute-start.12 = (bf16[6,192,128]{2,1,0:T(8,128)(2,1)S(1)}, bf16[6,192,128]{2,1,0:T(8,128)(2,1)S(1)}, u32[]{:S(2)}, u32[]{:S(2)}) collective-permute-start(bf16[6,192,128]{2,1,0:T(8,128)(2,1)S(1)} %compose.3), channel_id=1, source_target_pairs={{0,16},{4,20},{8,24},{12,28},{16,0},{20,4},{24,8},{28,12},{1,17},{... | collective-permute-start | bytes 884744 | tf_op jit(solution)/shard_map/ppermute | solution.py:37
  53.8 13.7 %collective-permute-done.12.refs_2_ = bf16[6,192,128]{2,1,0:T(8,128)(2,1)S(1)} collective-permute-done((bf16[6,192,128]{2,1,0:T(8,128)(2,1)S(1)}, bf16[6,192,128]{2,1,0:T(8,128)(2,1)S(1)}, u32[]{:S(2)}, u32[]{:S(2)}) %collective-permute-start.12) | collective-permute-done | bytes 294944 | tf_op jit(solution)/shard_map/ppermute | solution.py:37
  67.5 4.0 %resolve.1 = (bf16[6,32,128]{2,1,0:T(8,128)(2,1)S(1)}, bf16[6,32,128]{2,1,0:T(8,128)(2,1)S(1)}, bf16[6,32,128]{2,1,0:T(8,128)(2,1)S(1)}, bf16[6,32,128]{2,1,0:T(8,128)(2,1)S(1)}) custom-call(s32[1]{0:T(128)} %bitcast.place, s32[1]{0:T(128)} %bitcast.5.line, bf16[4,4,256,256]{3,2,1,0:T(8,128)(2,1)S(1)} %get-tuple-element.22.refs_0_, ...), custom_call_target="tpu_custom_call" | custom-call | tf_op jit(solution)/shard_map/resolve/pallas_call | solution.py:355
  71.6 1.0 %collective-permute-start.14 = (bf16[6,32,128]{2,1,0:T(8,128)(2,1)S(1)}, bf16[6,32,128]{2,1,0:T(8,128)(2,1)S(1)}, u32[]{:S(2)}, u32[]{:S(2)}) collective-permute-start(bf16[6,32,128]{2,1,0:T(8,128)(2,1)S(1)} %get-tuple-element.27), channel_id=1, source_target_pairs={{0,2},{1,3},{2,0},{3,1},{4,6},{5,7},{6,4},{7,5},{8,10},{9,11},{10,... | collective-permute-start | bytes 147464 | tf_op jit(solution)/shard_map/ppermute | solution.py:37
  72.5 0.9 %collective-permute-start.15 = (bf16[6,32,128]{2,1,0:T(8,128)(2,1)S(1)}, bf16[6,32,128]{2,1,0:T(8,128)(2,1)S(1)}, u32[]{:S(2)}, u32[]{:S(2)}) collective-permute-start(bf16[6,32,128]{2,1,0:T(8,128)(2,1)S(1)} %get-tuple-element.28), channel_id=1, source_target_pairs={{0,3},{1,2},{2,1},{3,0},{4,7},{5,6},{6,5},{7,4},{8,11},{9,10},{10,... | collective-permute-start | bytes 147464 | tf_op jit(solution)/shard_map/ppermute | solution.py:37
  73.4 2.5 %collective-permute-done.14.refs_2_ = bf16[6,32,128]{2,1,0:T(8,128)(2,1)S(1)} collective-permute-done((bf16[6,32,128]{2,1,0:T(8,128)(2,1)S(1)}, bf16[6,32,128]{2,1,0:T(8,128)(2,1)S(1)}, u32[]{:S(2)}, u32[]{:S(2)}) %collective-permute-start.14) | collective-permute-done | bytes 49184 | tf_op jit(solution)/shard_map/ppermute | solution.py:37
  76.6 2.6 %finish.1 = bf16[4,512,128]{2,1,0:T(8,128)(2,1)} custom-call(s32[1]{0:T(128)} %bitcast.place, s32[4]{0:T(128)S(1)} %bitcast.14, bf16[4,512,512]{2,1,0:T(8,128)(2,1)S(1)} %bitcast.8, bf16[4,192,512]{2,1,0:T(8,128)(2,1)S(1)} %bitcast.10, bf16[4,512,128]{2,1,0:T(8,128)(2,1)S(1)} %bitcast.12, bf16[6,32,128]{2,1,0:T(8,128)(2,1)S(1)} %get-tuple-element.25.refs_0_, ...), custom_call_target="tpu_custom_call" | custom-call | tf_op jit(solution)/shard_map/finish/pallas_call | solution.py:355
  (30 shorter events, 2.5 us)
Async XLA Ops:
  0.0 1.6 %copy-start = (bf16[1,1,4,512,512]{4,3,2,1,0:T(8,128)(2,1)S(1)}, bf16[1,1,4,512,512]{4,3,2,1,0:T(8,128)(2,1)}, u32[]{:S(2)}) copy-start(bf16[1,1,4,512,512]{4,3,2,1,0:T(8,128)(2,1)} %param.5) | copy-start | bytes 6291460
  1.6 1.1 %copy-start.2 = (bf16[1,1,4,3,64,512]{5,4,3,2,1,0:T(8,128)(2,1)S(1)}, bf16[1,1,4,3,64,512]{5,4,3,2,1,0:T(8,128)(2,1)}, u32[]{:S(2)}) copy-start(bf16[1,1,4,3,64,512]{5,4,3,2,1,0:T(8,128)(2,1)} %param.6) | copy-start | bytes 2359300
  2.7 1.0 %copy-start.4 = (bf16[1,1,4,512,128]{4,3,2,1,0:T(8,128)(2,1)S(1)}, bf16[1,1,4,512,128]{4,3,2,1,0:T(8,128)(2,1)}, u32[]{:S(2)}) copy-start(bf16[1,1,4,512,128]{4,3,2,1,0:T(8,128)(2,1)} %param.4) | copy-start | bytes 1572868
  3.8 0.7 copy-start.6
  6.5 10.0 %collective-permute-start = (bf16[1152,128]{1,0:T(8,128)(2,1)S(1)}, bf16[1152,128]{1,0:T(8,128)(2,1)S(1)}, u32[]{:S(2)}, u32[]{:S(2)}) collective-permute-start(bf16[1152,128]{1,0:T(8,128)(2,1)S(1)} %get-tuple-element.17.refs_0_), channel_id=1, source_target_pairs={{0,2},{1,3},{2,0},{3,1},{4,6},{5,7},{6,4},{7,5},{8,10},{9,11},{10,... | collective-permute-start | bytes 884744 | tf_op jit(solution)/shard_map/ppermute | solution.py:37
  9.5 13.2 %collective-permute-start.1 = (bf16[1152,128]{1,0:T(8,128)(2,1)S(1)}, bf16[1152,128]{1,0:T(8,128)(2,1)S(1)}, u32[]{:S(2)}, u32[]{:S(2)}) collective-permute-start(bf16[1152,128]{1,0:T(8,128)(2,1)S(1)} %get-tuple-element.17.refs_0_), channel_id=1, source_target_pairs={{0,1},{1,0},{2,3},{3,2},{4,5},{5,4},{6,7},{7,6},{8,9},{9,8},{10,11... | collective-permute-start | bytes 884744 | tf_op jit(solution)/shard_map/ppermute | solution.py:37
  16.5 6.2 %collective-permute-start.2 = (bf16[1152,128]{1,0:T(8,128)(2,1)S(1)}, bf16[1152,128]{1,0:T(8,128)(2,1)S(1)}, u32[]{:S(2)}, u32[]{:S(2)}) collective-permute-start(bf16[1152,128]{1,0:T(8,128)(2,1)S(1)} %collective-permute-done.refs_1_), channel_id=1, source_target_pairs={{0,1},{1,0},{2,3},{3,2},{4,5},{5,4},{6,7},{7,6},{8,9},{9,8},{10,11... | collective-permute-start | bytes 884744 | tf_op jit(solution)/shard_map/ppermute | solution.py:37
  16.5 2.3 %collective-permute-start.3 = (bf16[6,32,128]{2,1,0:T(8,128)(2,1)S(1)}, bf16[6,32,128]{2,1,0:T(8,128)(2,1)S(1)}, u32[]{:S(2)}, u32[]{:S(2)}) collective-permute-start(bf16[6,32,128]{2,1,0:T(8,128)(2,1)S(1)} %get-tuple-element.19), channel_id=1, source_target_pairs={{0,1},{1,0},{2,3},{3,2},{4,5},{5,4},{6,7},{7,6},{8,9},{9,8},{10,11... | collective-permute-start | bytes 147464 | tf_op jit(solution)/shard_map/ppermute | solution.py:37
  17.1 4.1 %collective-permute-start.4 = (bf16[6,32,128]{2,1,0:T(8,128)(2,1)S(1)}, bf16[6,32,128]{2,1,0:T(8,128)(2,1)S(1)}, u32[]{:S(2)}, u32[]{:S(2)}) collective-permute-start(bf16[6,32,128]{2,1,0:T(8,128)(2,1)S(1)} %get-tuple-element.20), channel_id=1, source_target_pairs={{0,2},{1,3},{2,0},{3,1},{4,6},{5,7},{6,4},{7,5},{8,10},{9,11},{10,... | collective-permute-start | bytes 147464 | tf_op jit(solution)/shard_map/ppermute | solution.py:37
  18.8 3.9 %collective-permute-start.5 = (bf16[6,32,128]{2,1,0:T(8,128)(2,1)S(1)}, bf16[6,32,128]{2,1,0:T(8,128)(2,1)S(1)}, u32[]{:S(2)}, u32[]{:S(2)}) collective-permute-start(bf16[6,32,128]{2,1,0:T(8,128)(2,1)S(1)} %get-tuple-element.21), channel_id=1, source_target_pairs={{0,3},{1,2},{2,1},{3,0},{4,7},{5,6},{6,5},{7,4},{8,11},{9,10},{10,... | collective-permute-start | bytes 147464 | tf_op jit(solution)/shard_map/ppermute | solution.py:37
  27.8 9.0 %collective-permute-start.7 = (bf16[6,192,128]{2,1,0:T(8,128)(2,1)S(1)}, bf16[6,192,128]{2,1,0:T(8,128)(2,1)S(1)}, u32[]{:S(2)}, u32[]{:S(2)}) collective-permute-start(bf16[6,192,128]{2,1,0:T(8,128)(2,1)S(1)} %get-tuple-element.24.own), channel_id=1, source_target_pairs={{0,4},{4,0},{8,12},{12,8},{16,20},{20,16},{24,28},{28,24},{1,5},{5... | collective-permute-start | bytes 884744 | tf_op jit(solution)/shard_map/ppermute | solution.py:37
  29.4 7.4 %collective-permute-start.6 = (bf16[6,192,128]{2,1,0:T(8,128)(2,1)S(1)}, bf16[6,192,128]{2,1,0:T(8,128)(2,1)}, u32[]{:S(2)}, u32[]{:S(2)}) collective-permute-start(bf16[6,192,128]{2,1,0:T(8,128)(2,1)S(1)} %get-tuple-element.24.own), channel_id=1, source_target_pairs={{0,1},{1,0},{2,3},{3,2},{4,5},{5,4},{6,7},{7,6},{8,9},{9,8},{10,11... | collective-permute-start | bytes 884744 | tf_op jit(solution)/shard_map/ppermute | solution.py:37
  36.8 1.6 %collective-permute-start.8 = (bf16[6,192,128]{2,1,0:T(8,128)(2,1)S(1)}, bf16[6,192,128]{2,1,0:T(8,128)(2,1)S(1)}, u32[]{:S(2)}, u32[]{:S(2)}) collective-permute-start(bf16[6,192,128]{2,1,0:T(8,128)(2,1)S(1)} %collective-permute-done.7.got.refs_3_), channel_id=1, source_target_pairs={{0,1},{1,0},{2,3},{3,2},{4,5},{5,4},{6,7},{7,6},{8,9},{9,8},{10,11... | collective-permute-start | bytes 884744 | tf_op jit(solution)/shard_map/ppermute | solution.py:37
  39.8 9.1 %collective-permute-start.10 = (bf16[6,192,128]{2,1,0:T(8,128)(2,1)S(1)}, bf16[6,192,128]{2,1,0:T(8,128)(2,1)S(1)}, u32[]{:S(2)}, u32[]{:S(2)}) collective-permute-start(bf16[6,192,128]{2,1,0:T(8,128)(2,1)S(1)} %compose.2.own), channel_id=1, source_target_pairs={{0,8},{4,12},{8,0},{12,4},{16,24},{20,28},{24,16},{28,20},{1,9},{5... | collective-permute-start | bytes 884744 | tf_op jit(solution)/shard_map/ppermute | solution.py:37
  41.5 7.5 %collective-permute-start.9 = (bf16[6,192,128]{2,1,0:T(8,128)(2,1)S(1)}, bf16[6,192,128]{2,1,0:T(8,128)(2,1)S(1)}, u32[]{:S(2)}, u32[]{:S(2)}) collective-permute-start(bf16[6,192,128]{2,1,0:T(8,128)(2,1)S(1)} %compose.2.own), channel_id=1, source_target_pairs={{0,1},{1,0},{2,3},{3,2},{4,5},{5,4},{6,7},{7,6},{8,9},{9,8},{10,11... | collective-permute-start | bytes 884744 | tf_op jit(solution)/shard_map/ppermute | solution.py:37
  49.0 1.6 %collective-permute-start.11 = (bf16[6,192,128]{2,1,0:T(8,128)(2,1)S(1)}, bf16[6,192,128]{2,1,0:T(8,128)(2,1)S(1)}, u32[]{:S(2)}, u32[]{:S(2)}) collective-permute-start(bf16[6,192,128]{2,1,0:T(8,128)(2,1)S(1)} %collective-permute-done.10.got.refs_5_), channel_id=1, source_target_pairs={{0,1},{1,0},{2,3},{3,2},{4,5},{5,4},{6,7},{7,6},{8,9},{9,8},{10,11... | collective-permute-start | bytes 884744 | tf_op jit(solution)/shard_map/ppermute | solution.py:37
  51.1 25.5 %copy-start.1 = (bf16[1,1,4,512,512]{4,3,2,1,0:T(8,128)(2,1)S(1)}, bf16[1,1,4,512,512]{4,3,2,1,0:T(8,128)(2,1)}, u32[]{:S(2)}) copy-start(bf16[1,1,4,512,512]{4,3,2,1,0:T(8,128)(2,1)} %param.5) | copy-start | bytes 6291460
  51.1 25.5 %copy-start.3 = (bf16[1,1,4,3,64,512]{5,4,3,2,1,0:T(8,128)(2,1)S(1)}, bf16[1,1,4,3,64,512]{5,4,3,2,1,0:T(8,128)(2,1)}, u32[]{:S(2)}) copy-start(bf16[1,1,4,3,64,512]{5,4,3,2,1,0:T(8,128)(2,1)} %param.6) | copy-start | bytes 2359300
  51.1 25.5 %copy-start.5 = (bf16[1,1,4,512,128]{4,3,2,1,0:T(8,128)(2,1)S(1)}, bf16[1,1,4,512,128]{4,3,2,1,0:T(8,128)(2,1)}, u32[]{:S(2)}) copy-start(bf16[1,1,4,512,128]{4,3,2,1,0:T(8,128)(2,1)} %param.4) | copy-start | bytes 1572868
  51.1 25.5 %copy-start.7 = (s32[1,1,4]{2,1,0:T(1,128)S(1)}, s32[1,1,4]{2,1,0:T(1,128)}, u32[]{:S(2)}) copy-start(s32[1,1,4]{2,1,0:T(1,128)} %param.7) | copy-start | bytes 52
  51.1 16.3 %collective-permute-start.12 = (bf16[6,192,128]{2,1,0:T(8,128)(2,1)S(1)}, bf16[6,192,128]{2,1,0:T(8,128)(2,1)S(1)}, u32[]{:S(2)}, u32[]{:S(2)}) collective-permute-start(bf16[6,192,128]{2,1,0:T(8,128)(2,1)S(1)} %compose.3), channel_id=1, source_target_pairs={{0,16},{4,20},{8,24},{12,28},{16,0},{20,4},{24,8},{28,12},{1,17},{... | collective-permute-start | bytes 884744 | tf_op jit(solution)/shard_map/ppermute | solution.py:37
  71.5 1.9 %collective-permute-start.13 = (bf16[6,32,128]{2,1,0:T(8,128)(2,1)S(1)}, bf16[6,32,128]{2,1,0:T(8,128)(2,1)S(1)}, u32[]{:S(2)}, u32[]{:S(2)}) collective-permute-start(bf16[6,32,128]{2,1,0:T(8,128)(2,1)S(1)} %get-tuple-element.26), channel_id=1, source_target_pairs={{0,1},{1,0},{2,3},{3,2},{4,5},{5,4},{6,7},{7,6},{8,9},{9,8},{10,11... | collective-permute-start | bytes 147464 | tf_op jit(solution)/shard_map/ppermute | solution.py:37
  71.6 4.3 %collective-permute-start.14 = (bf16[6,32,128]{2,1,0:T(8,128)(2,1)S(1)}, bf16[6,32,128]{2,1,0:T(8,128)(2,1)S(1)}, u32[]{:S(2)}, u32[]{:S(2)}) collective-permute-start(bf16[6,32,128]{2,1,0:T(8,128)(2,1)S(1)} %get-tuple-element.27), channel_id=1, source_target_pairs={{0,2},{1,3},{2,0},{3,1},{4,6},{5,7},{6,4},{7,5},{8,10},{9,11},{10,... | collective-permute-start | bytes 147464 | tf_op jit(solution)/shard_map/ppermute | solution.py:37
  72.5 4.0 %collective-permute-start.15 = (bf16[6,32,128]{2,1,0:T(8,128)(2,1)S(1)}, bf16[6,32,128]{2,1,0:T(8,128)(2,1)S(1)}, u32[]{:S(2)}, u32[]{:S(2)}) collective-permute-start(bf16[6,32,128]{2,1,0:T(8,128)(2,1)S(1)} %get-tuple-element.28), channel_id=1, source_target_pairs={{0,3},{1,2},{2,1},{3,0},{4,7},{5,6},{6,5},{7,4},{8,11},{9,10},{10,... | collective-permute-start | bytes 147464 | tf_op jit(solution)/shard_map/ppermute | solution.py:37
